TPU v7x, 32 devices: a whole 2x2x4 slice. The times are simulated.
32 devices in a mesh: dp: 4 (over z), fsdp: 8 (over y, x, core).
Axes of the slice: x: 2, y: 2, z: 4, core: 2. Of those that a mesh axis runs over, the one named last changes fastest.
Arguments:
- embed_table: bfloat16 [8192, 128], P(('dp', 'fsdp')), may hold values from -43 to 43
- token_ids: int32 [16384], P(('dp', 'fsdp')), may hold values from 0 to 8191
- time_steps: int32 [16384], P(('dp', 'fsdp')), may hold values from 0 to 1999, as said below
- segment_ids: int32 [16384], P(('dp', 'fsdp')), may hold values from 0 to 7, as said below
- noise_draw: bfloat16 [16384, 128], P(('dp', 'fsdp')), may hold values from -6 to 6
- w_up: bfloat16 [128, 768], P(None, ('dp', 'fsdp')), may hold values from -0.5 to 0.5
- w_time: bfloat16 [128, 768], P(None, ('dp', 'fsdp')), may hold values from -0.5 to 0.5
- w_qkv: bfloat16 [768, 2304], P(None, ('dp', 'fsdp')), may hold values from -0.21875 to 0.21875
- w_out: bfloat16 [768, 768], P(None, ('dp', 'fsdp')), may hold values from -0.875 to 0.875
- w_in: bfloat16 [768, 3072], P(None, ('dp', 'fsdp')), may hold values from -0.21875 to 0.21875
- w_down: bfloat16 [3072, 768], P(('dp', 'fsdp')), may hold values from -0.109375 to 0.109375
- gain_one: bfloat16 [768], P(('dp', 'fsdp')), may hold values from 0.099609375 to 1.8984375
- gain_two: bfloat16 [768], P(('dp', 'fsdp')), may hold values from 0.099609375 to 1.8984375
- cotangent: bfloat16 [16384, 768], P(('dp', 'fsdp')), may hold values from -6 to 6
Outputs:
- output: bfloat16 [16384, 768], P(('dp', 'fsdp'))
- table_grad: float32 [8192, 128], P(('dp', 'fsdp'))
- noise_grad: float32 [16384, 128], P(('dp', 'fsdp'))
- up_grad: float32 [128, 768], P(None, ('dp', 'fsdp'))
- time_grad: float32 [128, 768], P(None, ('dp', 'fsdp'))
- qkv_grad: float32 [768, 2304], P(None, ('dp', 'fsdp'))
- out_grad: float32 [768, 768], P(None, ('dp', 'fsdp'))
- in_grad: float32 [768, 3072], P(None, ('dp', 'fsdp'))
- down_grad: float32 [3072, 768], P(('dp', 'fsdp'))
- gain_one_grad: float32 [768], P(('dp', 'fsdp'))
- gain_two_grad: float32 [768], P(('dp', 'fsdp'))
Inputs may be any that keep to these rules, and one draw needn't show every extreme that they name: `segment_ids`: the tokens of each device are whole items: in every aligned block of 512 tokens the ids are either all 0 (one item) or count items of 64 tokens from 0 in order; both kinds of block occur in every draw. `time_steps`: all tokens of one item have the same time step.
All inputs are finite; a program needn't handle non-finite values.
Results may differ from a plain program's by a relative error of at most 0.014.
Values may be sent and summed in bfloat16 or wider, within the bound.
A program may use at most 128 MiB of HBM per device.

v0:
```python
import math

import jax
import jax.numpy as jnp
from jax import lax
from jax.sharding import PartitionSpec as P

HEADS = 12
HEAD_DIM = 64
EMBED = 128
VOCAB = 8192
TIME_DIM = 128
STEPS = 2000


def layer_norm(values, gain):
    center = values - jnp.mean(values, axis=1, keepdims=True)
    spread = jnp.mean(center * center, axis=1, keepdims=True)
    return center * lax.rsqrt(spread + 1e-05) * gain


def matmul(left, right):
    return jnp.dot(left, right, preferred_element_type=jnp.float32)


def matmul_left(left, right):
    return lax.dot_general(
        left, right, (((0,), (0,)), ((), ())), preferred_element_type=jnp.float32
    )


def matmul_right(left, right):
    return lax.dot_general(
        left, right, (((1,), (1,)), ((), ())), preferred_element_type=jnp.float32
    )


def gelu_exact(values):
    return jax.nn.gelu(values, approximate=False)


def time_features(time_steps):
    half_dim = TIME_DIM // 2
    frequency = jnp.exp(-math.log(10000.0) * jnp.arange(half_dim, dtype=jnp.float32) / half_dim)
    angles = time_steps.astype(jnp.float32)[:, None] * frequency[None, :]
    return jnp.concatenate([jnp.sin(angles), jnp.cos(angles)], axis=1)


def block_scores(q_block, k_heads, seg_block, seg_whole):
    scores = jnp.einsum("qhd,khd->hqk", q_block, k_heads, preferred_element_type=jnp.float32) * (
        1.0 / math.sqrt(HEAD_DIM)
    )
    allowed = seg_block[:, None] == seg_whole[None, :]
    return jnp.where(allowed[None], scores, -1e30)


def attention_forward(query_part, key_part, value_part, segments):
    row_count = query_part.shape[0]
    q_heads = query_part.reshape(row_count, HEADS, HEAD_DIM)
    k_heads = key_part.reshape(row_count, HEADS, HEAD_DIM)
    v_heads = value_part.reshape(row_count, HEADS, HEAD_DIM)
    scores = block_scores(q_heads, k_heads, segments, segments)
    row_peak = jnp.max(scores, axis=2, keepdims=True)
    weights = jnp.exp(scores - row_peak)
    row_total = jnp.sum(weights, axis=2, keepdims=True)
    soft_probs = (weights / row_total).astype(jnp.bfloat16)
    contexts = jnp.einsum("hqk,khd->qhd", soft_probs, v_heads, preferred_element_type=jnp.float32)
    log_totals = row_peak + jnp.log(row_total)
    context = contexts.reshape(row_count, HEADS * HEAD_DIM).astype(jnp.bfloat16)
    return (context, log_totals)


def attention_backward(query_part, key_part, value_part, segments, log_total, grad_context):
    row_count = query_part.shape[0]
    score_scale = 1.0 / math.sqrt(HEAD_DIM)
    q_heads = query_part.reshape(row_count, HEADS, HEAD_DIM)
    k_heads = key_part.reshape(row_count, HEADS, HEAD_DIM)
    v_heads = value_part.reshape(row_count, HEADS, HEAD_DIM)
    g_heads = grad_context.reshape(row_count, HEADS, HEAD_DIM)
    scores = block_scores(q_heads, k_heads, segments, segments)
    soft_probs = jnp.exp(scores - log_total)
    probs_low = soft_probs.astype(jnp.bfloat16)
    grad_probs = jnp.einsum("qhd,khd->hqk", g_heads, v_heads, preferred_element_type=jnp.float32)
    grad_value = jnp.einsum("hqk,qhd->khd", probs_low, g_heads, preferred_element_type=jnp.float32)
    grad_scores = soft_probs * (
        grad_probs - jnp.sum(soft_probs * grad_probs, axis=2, keepdims=True)
    )
    grad_scores = grad_scores.astype(jnp.bfloat16)
    query_pieces = (
        jnp.einsum("hqk,khd->qhd", grad_scores, k_heads, preferred_element_type=jnp.float32)
        * score_scale
    )
    grad_key = (
        jnp.einsum("hqk,qhd->khd", grad_scores, q_heads, preferred_element_type=jnp.float32)
        * score_scale
    )
    grad_query = query_pieces.reshape(row_count, HEADS * HEAD_DIM).astype(jnp.bfloat16)
    grad_key = grad_key.reshape(row_count, HEADS * HEAD_DIM).astype(jnp.bfloat16)
    grad_value = grad_value.reshape(row_count, HEADS * HEAD_DIM).astype(jnp.bfloat16)
    return (grad_query, grad_key, grad_value)


def local(
    embed_table,
    token_ids,
    time_steps,
    segment_ids,
    noise_draw,
    w_up,
    w_time,
    w_qkv,
    w_out,
    w_in,
    w_down,
    gain_one,
    gain_two,
    cotangent,
):
    table_values = embed_table.astype(jnp.float32)
    norm_values = jnp.sqrt(jnp.sum(table_values * table_values, axis=1) + 1e-06)
    norm_total = lax.psum(jnp.sum(norm_values), ("dp", "fsdp"))
    mean_norm = norm_total / VOCAB
    factor = math.sqrt(EMBED) / mean_norm
    gathered = (
        lax.all_gather(embed_table, ("dp", "fsdp"), axis=0, tiled=True),
        lax.all_gather(w_up, ("dp", "fsdp"), axis=1, tiled=True),
        lax.all_gather(w_time, ("dp", "fsdp"), axis=1, tiled=True),
        lax.all_gather(w_qkv, ("dp", "fsdp"), axis=1, tiled=True),
        lax.all_gather(w_out, ("dp", "fsdp"), axis=1, tiled=True),
        lax.all_gather(w_in, ("dp", "fsdp"), axis=1, tiled=True),
        lax.all_gather(w_down, ("dp", "fsdp"), axis=0, tiled=True),
        lax.all_gather(gain_one, ("dp", "fsdp"), axis=0, tiled=True),
        lax.all_gather(gain_two, ("dp", "fsdp"), axis=0, tiled=True),
    )
    (
        full_table,
        up_full,
        time_full,
        qkv_full,
        out_full,
        in_full,
        down_full,
        gain_first,
        gain_second,
    ) = gathered
    raw_rows = jnp.take(full_table, token_ids, axis=0).astype(jnp.float32)
    level_value = time_steps.astype(jnp.float32) / STEPS + 0.0001
    signal = jnp.sqrt(1.0 - jnp.sqrt(level_value))
    blur_level = jnp.sqrt(jnp.sqrt(level_value))
    noisy_input = (
        signal[:, None] * (raw_rows * factor) + blur_level[:, None] * noise_draw.astype(jnp.float32)
    ).astype(jnp.bfloat16)
    time_feats = time_features(time_steps).astype(jnp.bfloat16)
    embedded = matmul(noisy_input, up_full) + matmul(time_feats, time_full)
    normed = layer_norm(embedded, gain_first.astype(jnp.float32)).astype(jnp.bfloat16)
    mixed_qkv = matmul(normed, qkv_full)
    width = mixed_qkv.shape[1] // 3
    query_part = mixed_qkv[:, :width].astype(jnp.bfloat16)
    key_part = mixed_qkv[:, width : 2 * width].astype(jnp.bfloat16)
    value_part = mixed_qkv[:, 2 * width :].astype(jnp.bfloat16)
    context, log_total = attention_forward(query_part, key_part, value_part, segment_ids)
    middle = embedded + matmul(context, out_full)
    normed_two = layer_norm(middle, gain_second.astype(jnp.float32)).astype(jnp.bfloat16)
    pre_act = matmul(normed_two, in_full)
    activated = gelu_exact(pre_act).astype(jnp.bfloat16)
    output = (middle + matmul(activated, down_full)).astype(jnp.bfloat16)
    again = (
        lax.all_gather(w_up, ("dp", "fsdp"), axis=1, tiled=True),
        lax.all_gather(w_time, ("dp", "fsdp"), axis=1, tiled=True),
        lax.all_gather(w_qkv, ("dp", "fsdp"), axis=1, tiled=True),
        lax.all_gather(w_out, ("dp", "fsdp"), axis=1, tiled=True),
        lax.all_gather(w_in, ("dp", "fsdp"), axis=1, tiled=True),
        lax.all_gather(w_down, ("dp", "fsdp"), axis=0, tiled=True),
        lax.all_gather(gain_one, ("dp", "fsdp"), axis=0, tiled=True),
        lax.all_gather(gain_two, ("dp", "fsdp"), axis=0, tiled=True),
    )
    up_back, time_back, qkv_back, out_back, in_back, down_back, gain_third, gain_fourth = again
    grad_down = matmul_left(activated, cotangent)
    grad_act = matmul_right(cotangent, down_back)
    unused_gelu, gelu_pull = jax.vjp(gelu_exact, pre_act)
    grad_pre = gelu_pull(grad_act)[0].astype(jnp.bfloat16)
    grad_in = matmul_left(normed_two, grad_pre)
    grad_normed_two = matmul_right(grad_pre, in_back)
    unused_second, second_pull = jax.vjp(layer_norm, middle, gain_fourth.astype(jnp.float32))
    grad_middle_norm, grad_gain_two = second_pull(grad_normed_two)
    grad_middle = cotangent.astype(jnp.float32) + grad_middle_norm
    mlp_shards = (
        lax.psum_scatter(grad_in, ("dp", "fsdp"), scatter_dimension=1, tiled=True),
        lax.psum_scatter(grad_down, ("dp", "fsdp"), scatter_dimension=0, tiled=True),
        lax.psum_scatter(grad_gain_two, ("dp", "fsdp"), scatter_dimension=0, tiled=True),
    )
    grad_branch = grad_middle.astype(jnp.bfloat16)
    grad_out = matmul_left(context, grad_branch)
    grad_context = matmul_right(grad_branch, out_back).astype(jnp.bfloat16)
    grad_query, grad_key, grad_value = attention_backward(
        query_part, key_part, value_part, segment_ids, log_total, grad_context
    )
    grad_mixed = jnp.concatenate([grad_query, grad_key, grad_value], axis=1)
    grad_qkv = matmul_left(normed, grad_mixed)
    grad_normed = matmul_right(grad_mixed, qkv_back)
    unused_first, first_pull = jax.vjp(layer_norm, embedded, gain_third.astype(jnp.float32))
    grad_embed_norm, grad_gain_one = first_pull(grad_normed)
    grad_embedded = (grad_middle + grad_embed_norm).astype(jnp.bfloat16)
    grad_up = matmul_left(noisy_input, grad_embedded)
    grad_time = matmul_left(time_feats, grad_embedded)
    grad_noisy = matmul_right(grad_embedded, up_back)
    noise_grad = blur_level[:, None] * grad_noisy
    grad_rows = signal[:, None] * grad_noisy
    counted = jnp.zeros((VOCAB, EMBED), jnp.float32).at[token_ids].add(grad_rows)
    rest_shards = (
        lax.psum_scatter(counted, ("dp", "fsdp"), scatter_dimension=0, tiled=True),
        lax.psum_scatter(grad_up, ("dp", "fsdp"), scatter_dimension=1, tiled=True),
        lax.psum_scatter(grad_time, ("dp", "fsdp"), scatter_dimension=1, tiled=True),
        lax.psum_scatter(grad_qkv, ("dp", "fsdp"), scatter_dimension=1, tiled=True),
        lax.psum_scatter(grad_out, ("dp", "fsdp"), scatter_dimension=1, tiled=True),
        lax.psum_scatter(grad_gain_one, ("dp", "fsdp"), scatter_dimension=0, tiled=True),
    )
    counted_own, up_own, time_own, qkv_own, out_own, gain_one_own = rest_shards
    in_own, down_own, gain_two_own = mlp_shards
    table_grad = factor * counted_own
    return (
        output,
        table_grad,
        noise_grad,
        up_own,
        time_own,
        qkv_own,
        out_own,
        in_own,
        down_own,
        gain_one_own,
        gain_two_own,
    )


def solution(mesh):
    in_specs = (
        P(("dp", "fsdp"), None),
        P(("dp", "fsdp")),
        P(("dp", "fsdp")),
        P(("dp", "fsdp")),
        P(("dp", "fsdp"), None),
        P(None, ("dp", "fsdp")),
        P(None, ("dp", "fsdp")),
        P(None, ("dp", "fsdp")),
        P(None, ("dp", "fsdp")),
        P(None, ("dp", "fsdp")),
        P(("dp", "fsdp"), None),
        P(("dp", "fsdp")),
        P(("dp", "fsdp")),
        P(("dp", "fsdp"), None),
    )
    out_specs = (
        P(("dp", "fsdp"), None),
        P(("dp", "fsdp"), None),
        P(("dp", "fsdp"), None),
        P(None, ("dp", "fsdp")),
        P(None, ("dp", "fsdp")),
        P(None, ("dp", "fsdp")),
        P(None, ("dp", "fsdp")),
        P(None, ("dp", "fsdp")),
        P(("dp", "fsdp"), None),
        P(("dp", "fsdp")),
        P(("dp", "fsdp")),
    )
    return jax.shard_map(local, mesh=mesh, in_specs=in_specs, out_specs=out_specs, check_vma=False)
```

profile of v0, /device:TPU:0, one launch (start us, length us, event | category | flops | bytes accessed | tf_op | source)
XLA Modules:
  0.0 1248.5 jit_solution(1002044045899057185)
XLA Ops:
  12.2 42.3 %psum.7 = f32[]{:T(128)} all-reduce(f32[]{:T(128)} %sqrt_reduce_fusion), channel_id=1, replica_groups=mesh['dp'=4,'fsdp'=8] {'dp','fsdp'}, use_global_device_ids=true, to_apply=%region_2.0 | all-reduce | flops 1 | bytes 8 | tf_op jit(solution)/shard_map/psum | solution.py:121
  56.8 40.5 %all-reduce.7 = (bf16[768]{0:T(1024)(128)(2,1)S(1)}, bf16[768]{0:T(1024)(128)(2,1)S(1)}) all-reduce(bf16[768]{0:T(1024)(128)(2,1)S(1)} %dynamic-update-slice, bf16[768]{0:T(1024)(128)(2,1)S(1)} %dynamic-update-slice.1), channel_id=1, replica_groups=mesh['dp'=4,'fsdp'=8] {'dp','fsdp'}, use_global_device_ids=true, to_apply=%add | all-reduce | flops 1536 | bytes 6144
  98.1 41.9 %all_gather.35 = bf16[128,768]{0,1:T(8,128)(2,1)S(1)} all-gather(bf16[128,24]{0,1:T(8,128)(2,1)} %param.19), channel_id=1, replica_groups=mesh['dp'=4,'fsdp'=8] {'dp','fsdp'}, dimensions={1}, use_global_device_ids=true | all-gather | bytes 202752 | tf_op jit(solution)/shard_map/all_gather | solution.py:126
  139.9 37.5 %all_gather.36 = bf16[128,768]{0,1:T(8,128)(2,1)S(1)} all-gather(bf16[128,24]{0,1:T(8,128)(2,1)} %param.20), channel_id=1, replica_groups=mesh['dp'=4,'fsdp'=8] {'dp','fsdp'}, dimensions={1}, use_global_device_ids=true | all-gather | bytes 202752 | tf_op jit(solution)/shard_map/all_gather | solution.py:127
  181.2 3.1 gather_fusion
  184.3 1.5 fusion.39
  186.7 4.1 convolution_convert_fusion
  190.9 1.3 fusion.45
  192.5 1.7 copy.54
  194.2 2.6 copy.53
  196.8 2.1 fusion.12
  198.9 2.6 fusion
  201.5 1.9 copy-done
  203.4 4.4 fusion.18
  207.8 2.4 fusion.47
  210.6 42.5 %all-gather.12.cloned.1.call-done = bf16[768,3072]{0,1:T(8,128)(2,1)} async-done(((bf16[768,96]{0,1:T(8,128)(2,1)}), bf16[768,3072]{0,1:T(8,128)(2,1)}) %all-gather.12.cloned.1.call-update) | async-done | bytes 4718608 | tf_op jit(solution)/shard_map/all_gather | solution.py:130
  253.1 7.4 fusion.41
  260.5 57.3 %all-gather.14.cloned.1.call-done = bf16[3072,768]{1,0:T(8,128)(2,1)} async-done(((bf16[96,768]{1,0:T(8,128)(2,1)}), bf16[3072,768]{1,0:T(8,128)(2,1)}) %all-gather.14.cloned.1.call-update) | async-done | bytes 4718608 | tf_op jit(solution)/shard_map/all_gather | solution.py:131
  317.8 19.5 %add_convert_fusion = (bf16[512,3072]{1,0:T(8,128)(2,1)S(1)}, f32[512,3072]{1,0:T(8,128)}) fusion(f32[512,3072]{1,0:T(8,128)} %fusion.41, bf16[512,768]{1,0:T(8,128)(2,1)} %param.27, bf16[3072,768]{1,0:T(8,128)(2,1)} %all-gather.14.cloned.1.call-done), kind=kOutput, calls=%fused_computation.14 | convolution fusion | flops 2529165312 | bytes 21233664 | tf_op jit(solution)/shard_map/dot_general | solution.py:33
  337.3 3.3 multiply_reduce_fusion.1
  341.3 1.2 copy-done.1
  343.7 1.7 convolution_convert_fusion.1
  345.4 2.4 copy.57
  347.7 9.0 fusion.15
  356.7 9.6 multiply_reduce_fusion
  366.3 7.2 multiply_convert_fusion
  373.6 2.0 multiply_convert_fusion.2
  376.8 1.4 copy-done.48
  378.4 2.9 multiply_reduce_fusion.2
  385.3 4.8 scatter_custom_fusion
  390.2 2.7 fusion.38
  393.0 2.4 fusion.26
  395.4 3.6 fusion.48
  399.1 6.7 fusion.20
  406.1 8.3 fusion.40
  414.5 6.2 multiply_convert_fusion.1
  420.7 1.6 copy-done.16
  422.4 5.1 fusion.49
  428.1 39.3 %all-reduce.6 = (f32[768]{0:T(1024)S(1)}, f32[768]{0:T(1024)S(1)}) all-reduce(f32[768]{0:T(1024)S(1)} %copy-done.46, f32[768]{0:T(1024)S(1)} %copy-done.45), channel_id=9, replica_groups=mesh['dp'=4,'fsdp'=8] {'dp','fsdp'}, use_global_device_ids=true, to_apply=%region_23.24.clone | all-reduce | flops 1536 | bytes 12288
  468.6 6.8 add_convert_fusion.2
  475.4 56.3 %reduce-scatter.12.cloned.1.call-done = f32[256,128]{1,0:T(8,128)} async-done(((f32[8192,128]{1,0:T(8,128)}), f32[256,128]{1,0:T(8,128)}) %reduce-scatter.12.cloned.1.call-update) | async-done | bytes 131088 | tf_op jit(solution)/shard_map/reduce_scatter | solution.py:211
  531.8 1.6 broadcast_multiply_fusion.1
  533.3 95.4 %reduce-scatter.22.cloned.1.call-done = f32[128,24]{0,1:T(8,128)} async-done(((f32[128,768]{0,1:T(8,128)}), f32[128,24]{0,1:T(8,128)}) %reduce-scatter.22.cloned.1.call-update) | async-done | bytes 12304
  628.8 100.2 %reduce-scatter.24.cloned.1.call-done = f32[128,24]{0,1:T(8,128)} async-done(((f32[128,768]{0,1:T(8,128)}), f32[128,24]{0,1:T(8,128)}) %reduce-scatter.24.cloned.1.call-update) | async-done | bytes 12304
  729.0 104.6 %reduce-scatter.16.cloned.1.call-done = f32[768,24]{0,1:T(8,128)} async-done(((f32[768,768]{0,1:T(8,128)}), f32[768,24]{0,1:T(8,128)}) %reduce-scatter.16.cloned.1.call-update) | async-done | bytes 73744 | tf_op jit(solution)/shard_map/reduce_scatter | solution.py:215
  833.6 124.6 %reduce-scatter.14.cloned.1.call-done = f32[768,72]{0,1:T(8,128)} async-done(((f32[768,2304]{0,1:T(8,128)}), f32[768,72]{0,1:T(8,128)}) %reduce-scatter.14.cloned.1.call-update) | async-done | bytes 221200 | tf_op jit(solution)/shard_map/reduce_scatter | solution.py:214
  958.2 141.7 %reduce-scatter.18.cloned.1.call-done = f32[768,96]{0,1:T(8,128)} async-done(((f32[768,3072]{0,1:T(8,128)}), f32[768,96]{0,1:T(8,128)}) %reduce-scatter.18.cloned.1.call-update) | async-done | bytes 294928 | tf_op jit(solution)/shard_map/reduce_scatter | solution.py:188
  1099.9 141.5 %reduce-scatter.20.cloned.1.call-done = f32[96,768]{1,0:T(8,128)} async-done(((f32[3072,768]{1,0:T(8,128)}), f32[96,768]{1,0:T(8,128)}) %reduce-scatter.20.cloned.1.call-update) | async-done | bytes 294928 | tf_op jit(solution)/shard_map/reduce_scatter | solution.py:189
  (167 shorter events, 21.9 us)
Async XLA Ops:
  7.2 174.0 %all-gather.6.cloned.1.call-start = ((), (), s32[]{:S(2)}) async-start(), calls=%async_computation.7 | async-start | bytes 2162688 | tf_op jit(solution)/shard_map/all_gather | solution.py:125
  7.9 178.7 %all-gather.8.cloned.1.call-start = ((), (), s32[]{:S(2)}) async-start(), calls=%async_computation.8 | async-start | bytes 3649536 | tf_op jit(solution)/shard_map/all_gather | solution.py:128
  8.7 199.2 %all-gather.10.cloned.1.call-start = ((), (), s32[]{:S(2)}) async-start(), calls=%async_computation.9 | async-start | bytes 1216512 | tf_op jit(solution)/shard_map/all_gather | solution.py:129
  9.4 243.7 %all-gather.12.cloned.1.call-start = ((), (), s32[]{:S(2)}) async-start(), calls=%async_computation.10 | async-start | bytes 4866048 | tf_op jit(solution)/shard_map/all_gather | solution.py:130
  10.0 307.9 %all-gather.14.cloned.1.call-start = ((), (), s32[]{:S(2)}) async-start(), calls=%async_computation.11 | async-start | bytes 4866048 | tf_op jit(solution)/shard_map/all_gather | solution.py:131
  10.6 521.2 %reduce-scatter.12.cloned.1.call-start = ((), (), s32[]{:S(2)}) async-start(), calls=%async_computation.12 | async-start | bytes 4325376 | tf_op jit(solution)/shard_map/reduce_scatter | solution.py:211
  97.4 93.4 %copy-start.37 = (f32[768]{0:T(1024)}, f32[768]{0:T(1024)S(1)}, u32[]{:S(2)}) copy-start(f32[768]{0:T(1024)S(1)} %convert_element_type.105) | copy-start | bytes 9220
  139.9 50.8 %copy-start.18 = (bf16[128,768]{0,1:T(8,128)(2,1)}, bf16[128,768]{0,1:T(8,128)(2,1)S(1)}, u32[]{:S(2)}) copy-start(bf16[128,768]{0,1:T(8,128)(2,1)S(1)} %all_gather.35) | copy-start | bytes 589828
  178.2 8.1 copy-start.43
  178.9 11.9 copy-start.44
  179.6 11.2 copy-start.28
  179.6 11.2 copy-start.30
  180.1 10.7 copy-start.24
  180.2 10.7 copy-start.26
  184.3 6.6 copy-start.20
  186.3 4.6 copy-start.32
  186.6 4.3 copy-start.35
  186.6 4.3 copy-start.40
  192.5 6.4 copy-start.4
  194.2 4.7 copy-start.6
  198.9 4.5 copy-start
  198.9 4.5 copy-start.8
  317.8 19.5 %copy-start.47 = (bf16[768,3072]{0,1:T(8,128)(2,1)S(1)}, bf16[768,3072]{0,1:T(8,128)(2,1)}, u32[]{:S(2)}) copy-start(bf16[768,3072]{0,1:T(8,128)(2,1)} %all-gather.12.cloned.1.call-done) | copy-start | bytes 14155780
  337.3 3.4 copy-start.11
  340.7 3.0 copy-start.22
  347.7 9.0 copy-start.9
  347.7 9.0 copy-start.10
  347.7 18.6 %slice-start = ((s8[12582912]{0:T(1024)(128)(4,1)}), s8[4194304]{0:T(1024)(128)(4,1)S(1)}, s32[]{:S(2)}) async-start(s8[12582912]{0:T(1024)(128)(4,1)} %bitcast.50), calls=%async_computation.19 | async-start | bytes 8388608
  347.7 18.6 %slice-start.1 = ((s8[12582912]{0:T(1024)(128)(4,1)}), s8[4194304]{0:T(1024)(128)(4,1)S(1)}, s32[]{:S(2)}) async-start(s8[12582912]{0:T(1024)(128)(4,1)} %bitcast.50), calls=%async_computation.20 | async-start | bytes 8388608
  356.7 9.6 slice-start.2
  366.3 7.2 copy-start.7
  376.8 4.5 copy-start.17
  378.4 2.9 copy-start.36
  381.3 2.8 copy-start.19
  381.4 3.9 copy-start.29
  384.2 6.0 copy-start.21
  390.1 2.9 copy-start.25
  390.1 2.9 copy-start.27
  390.1 9.0 copy-start.34
  390.1 9.0 copy-start.39
  390.1 9.0 copy-start.42
  390.1 238.7 %reduce-scatter.22.cloned.1.call-start = ((), (), s32[]{:S(2)}) async-start(), calls=%async_computation.17 | async-start | bytes 405504
  392.9 336.1 %reduce-scatter.24.cloned.1.call-start = ((), (), s32[]{:S(2)}) async-start(), calls=%async_computation.18 | async-start | bytes 405504
  395.4 438.3 %reduce-scatter.16.cloned.1.call-start = ((), (), s32[]{:S(2)}) async-start(), calls=%async_computation.14 | async-start | bytes 2433024 | tf_op jit(solution)/shard_map/reduce_scatter | solution.py:215
  399.0 559.2 %reduce-scatter.14.cloned.1.call-start = ((), (), s32[]{:S(2)}) async-start(), calls=%async_computation.13 | async-start | bytes 7299072 | tf_op jit(solution)/shard_map/reduce_scatter | solution.py:214
  405.9 694.0 %reduce-scatter.18.cloned.1.call-start = ((), (), s32[]{:S(2)}) async-start(), calls=%async_computation.15 | async-start | bytes 9732096 | tf_op jit(solution)/shard_map/reduce_scatter | solution.py:188
  414.5 827.0 %reduce-scatter.20.cloned.1.call-start = ((), (), s32[]{:S(2)}) async-start(), calls=%async_computation.16 | async-start | bytes 9732096 | tf_op jit(solution)/shard_map/reduce_scatter | solution.py:189
  414.5 7.9 copy-start.14
  (17 other events, 25.8 us)
Sparse Core Ops, SparseCore 0:
  10.8 59.0 all-gather.5
  72.9 59.1 all-gather.7
  135.0 52.8 all-gather.9
  190.6 62.4 all-gather.11
  255.9 61.9 all-gather.13
  390.2 141.5 reduce-scatter.11
  537.3 91.4 reduce-scatter.21
  634.3 94.6 reduce-scatter.23
  734.9 98.7 reduce-scatter.15
  839.7 118.4 reduce-scatter.13
  964.7 135.1 reduce-scatter.17
  1106.2 135.1 reduce-scatter.19
where the time goes:
time: 1250 us
  waiting for transfers between devices  868 us (69%)
  blocking collectives  202 us (16%)
  matrix products  108 us (9%)
  other arithmetic  30.7 us (2%)
  local copies, waits for them, and re-layouts  24 us (2%)
  between operations  15.8 us (1%)
    unnamed x14, waiting for transfers between devices  199 us
    reduce_scatter x1, waiting for transfers between devices, local(): lax.psum_scatter(grad_in, ('dp', 'fsdp'), scatter_dimension=1, tiled=True)  142 us
    reduce_scatter x1, waiting for transfers between devices, local(): lax.psum_scatter(grad_down, ('dp', 'fsdp'), scatter_dimension=0, tiled=True)  142 us
    reduce_scatter x1, waiting for transfers between devices, local(): lax.psum_scatter(grad_qkv, ('dp', 'fsdp'), scatter_dimension=1, tiled=True)  125 us
    reduce_scatter x1, waiting for transfers between devices, local(): lax.psum_scatter(grad_out, ('dp', 'fsdp'), scatter_dimension=1, tiled=True)  105 us
    unnamed x2, blocking collectives  79.9 us
    all_gather x1, waiting for transfers between devices, local(): lax.all_gather(w_down, ('dp', 'fsdp'), axis=0, tiled=True)  57.3 us
    reduce_scatter x1, waiting for transfers between devices, local(): lax.psum_scatter(counted, ('dp', 'fsdp'), scatter_dimension=0, tiled=True)  56.3 us
  transfers between devices with their start and end apart: 12, of which 9 were waited for; matrix products, arithmetic and copies ran while one was open for 7% of the time, Pallas kernels for 0%

commit v1 on v0

--- a/solution.py
+++ b/solution.py
@@ -1,8 +1,11 @@
+import functools
 import math
 
 import jax
 import jax.numpy as jnp
 from jax import lax
+from jax.experimental import pallas as pl
+from jax.experimental.pallas import tpu as pltpu
 from jax.sharding import PartitionSpec as P
 
 HEADS = 12
@@ -100,7 +103,7 @@
     return (grad_query, grad_key, grad_value)
 
 
-def local(
+def native_local(
     embed_table,
     token_ids,
     time_steps,
@@ -233,6 +236,428 @@
     )
 
 
+MESH = pl.DeviceIdType.MESH
+
+
+class Grid:
+    def __init__(self, Z, F):
+        self.Z, self.F = Z, F
+        self.X = math.isqrt(F // 2); self.Y = F // 2 // self.X
+    def here(self):
+        z = lax.axis_index("dp"); f = lax.axis_index("fsdp")
+        return z, f // (2 * self.X), (f // 2) % self.X, f % 2
+    def dev(self, z, y, x, c):
+        return (z, (y * self.X + x) * 2 + c)
+
+def barrier(g):
+    z, y, x, c = g.here()
+    bar = pltpu.get_barrier_semaphore()
+    n = 0
+    peers = [g.dev((z + k) % g.Z, y, x, c) for k in range(1, g.Z)]
+    peers += [g.dev(z, (y + k) % g.Y, x, c) for k in range(1, g.Y)]
+    peers += [g.dev(z, y, (x + k) % g.X, c) for k in range(1, g.X)]
+    peers += [g.dev(z, y, x, 1 - c)]
+    for p in peers:
+        pl.semaphore_signal(bar, inc=1, device_id=p, device_id_type=MESH)
+    pl.semaphore_wait(bar, len(peers))
+
+class Gather:
+    def __init__(self, g, shard, full, cut, local_sem, send, recv):
+        self.g = g
+        r, C = shard.shape
+        self.r, self.C = r, C
+        self.shard = shard
+        self.full = full
+        kind, at = cut
+        if kind == "lane":
+            self.h = ((slice(None), pl.ds(0, at)), (slice(None), pl.ds(at, C - at)))
+        else:
+            self.h = ((pl.ds(0, at), slice(None)), (pl.ds(at, r - at), slice(None)))
+        self.local_sem, self.send, self.recv = local_sem, send, recv
+        self.i = 0
+        self.groups = {}
+    def cp(self, name, src, dst, dev):
+        c = pltpu.make_async_remote_copy(src_ref=src, dst_ref=dst, send_sem=self.send.at[self.i], recv_sem=self.recv.at[self.i], device_id=dev, device_id_type=MESH)
+        self.i += 1
+        c.start()
+        self.groups.setdefault(name, []).append(c)
+    def wait(self, name):
+        for c in self.groups[name]:
+            c.wait_recv()
+    def finish(self):
+        for cs in self.groups.values():
+            for c in cs: c.wait_send()
+    def s1(self):
+        g = self.g; z, y, x, c = g.here()
+        self.local = pltpu.make_async_copy(self.shard, self.full.at[z, y, x, c], self.local_sem)
+        self.local.start()
+        for k in range(1, g.Z):
+            self.cp("z", self.shard, self.full.at[z, y, x, c], g.dev((z + k) % g.Z, y, x, c))
+    def s2(self):
+        g = self.g; z, y, x, c = g.here()
+        self.local.wait()
+        self.wait("z")
+        a, b = self.h
+        for k in range(1, g.X):
+            v = self.full.at[:, y, x, c, a[0], a[1]]
+            self.cp("a2", v, v, g.dev(z, y, (x + k) % g.X, c))
+        for k in range(1, g.Y):
+            v = self.full.at[:, y, x, c, b[0], b[1]]
+            self.cp("b2", v, v, g.dev(z, (y + k) % g.Y, x, c))
+        v = self.full.at[:, y, x, c]
+        self.cp("sib1", v, v, g.dev(z, y, x, 1 - c))
+    def s3(self):
+        g = self.g; z, y, x, c = g.here()
+        self.wait("a2"); self.wait("b2")
+        a, b = self.h
+        for k in range(1, g.Y):
+            v = self.full.at[:, y, :, c, a[0], a[1]]
+            self.cp("a3", v, v, g.dev(z, (y + k) % g.Y, x, c))
+        for k in range(1, g.X):
+            v = self.full.at[:, :, x, c, b[0], b[1]]
+            self.cp("b3", v, v, g.dev(z, y, (x + k) % g.X, c))
+        sib = g.dev(z, y, x, 1 - c)
+        for k in range(1, g.X):
+            v = self.full.at[:, y, (x + g.X - k) % g.X, c, a[0], a[1]]
+            self.cp("sib2", v, v, sib)
+        for k in range(1, g.Y):
+            v = self.full.at[:, (y + g.Y - k) % g.Y, x, c, b[0], b[1]]
+            self.cp("sib2", v, v, sib)
+    def s4(self):
+        g = self.g; z, y, x, c = g.here()
+        self.wait("a3"); self.wait("b3")
+        a, b = self.h
+        sib = g.dev(z, y, x, 1 - c)
+        for k in range(1, g.Y):
+            v = self.full.at[:, (y + g.Y - k) % g.Y, :, c, a[0], a[1]]
+            self.cp("sib3", v, v, sib)
+        for k in range(1, g.X):
+            v = self.full.at[:, :, (x + g.X - k) % g.X, c, b[0], b[1]]
+            self.cp("sib3", v, v, sib)
+    def done(self):
+        self.wait("sib1"); self.wait("sib2"); self.wait("sib3")
+
+def n_copies(g):
+    return (g.Z - 1) + (g.X - 1) + (g.Y - 1) + 1 + 2 * (g.X - 1 + g.Y - 1) + (g.X - 1 + g.Y - 1)
+
+def ag_kernel(g, cuts, *refs):
+    n = len(cuts)
+    shards, fulls = refs[:n], refs[n:2 * n]
+    local, send, recv = refs[2 * n:]
+    barrier(g)
+    ts = [Gather(g, s, f, cut, local.at[i], send.at[i], recv.at[i]) for i, (s, f, cut) in enumerate(zip(shards, fulls, cuts))]
+    for t in ts: t.s1()
+    for tick in range(n + 3):
+        for st in (1, 2, 3, 4):
+            i = tick - (st - 1)
+            if 0 <= i < n:
+                (ts[i].s2, ts[i].s3, ts[i].s4, ts[i].done)[st - 1]()
+    for t in ts: t.finish()
+
+def gather_all(g, shards, cuts, space):
+    n = len(shards)
+    outs = tuple(jax.ShapeDtypeStruct((g.Z, g.Y, g.X, 2, *s.shape), s.dtype) for s in shards)
+    nc = n_copies(g)
+    fulls = pl.pallas_call(
+        functools.partial(ag_kernel, g, cuts),
+        out_shape=outs,
+        in_specs=[pl.BlockSpec(memory_space=pltpu.VMEM)] * n,
+        out_specs=tuple([pl.BlockSpec(memory_space=space)] * n),
+        scratch_shapes=[pltpu.SemaphoreType.DMA((n,)), pltpu.SemaphoreType.DMA((n, nc)), pltpu.SemaphoreType.DMA((n, nc))],
+        compiler_params=pltpu.CompilerParams(collective_id=0, has_side_effects=True, vmem_limit_bytes=60 * 2**20),
+        name="gather_weights",
+    )(*shards)
+    return [f.reshape(g.Z * g.F * s.shape[0], s.shape[1]) for f, s in zip(fulls, shards)]
+
+
+def halves(r, C, cut):
+    kind, at = cut
+    if kind == "lane":
+        return ((pl.ds(0, r), pl.ds(0, at)), (pl.ds(0, r), pl.ds(at, C - at)))
+    return ((pl.ds(0, at), pl.ds(0, C)), (pl.ds(at, r - at), pl.ds(0, C)))
+
+
+def half_shapes(r, C, cut):
+    kind, at = cut
+    return ((r, at), (r, C - at)) if kind == "lane" else ((at, C), (r - at, C))
+
+
+class Scatter:
+    def __init__(self, g, part, out, cut, bufs, send, recv):
+        self.g, self.out = g, out
+        self.part = part
+        r, C = part.shape[-2:]
+        self.a, self.b = halves(r, C, cut)
+        self.sib, self.r1a, self.r1b, self.r2a, self.r2b, self.r3 = bufs
+        self.send, self.recv = send, recv
+        self.i = 0
+        self.groups = {}
+
+    def copy(self, name, src, dst, dev):
+        c = pltpu.make_async_remote_copy(
+            src_ref=src, dst_ref=dst, send_sem=self.send.at[self.i], recv_sem=self.recv.at[self.i],
+            device_id=dev, device_id_type=MESH,
+        )
+        self.i += 1
+        c.start()
+        self.groups.setdefault(name, []).append(c)
+
+    def wait(self, name):
+        for c in self.groups.get(name, []):
+            c.wait_recv()
+
+    def finish(self):
+        for cs in self.groups.values():
+            for c in cs:
+                c.wait_send()
+
+    def s0(self):
+        g = self.g
+        z, y, x, c = g.here()
+        self.copy("sib", self.part.at[:, :, :, 1 - c], self.sib, g.dev(z, y, x, 1 - c))
+
+    def s1(self):
+        g = self.g
+        z, y, x, c = g.here()
+        self.wait("sib")
+
+        def add(i, carry):
+            iz, iy, ix = i // (g.Y * g.X), (i // g.X) % g.Y, i % g.X
+            self.part[iz, iy, ix, c] = self.part[iz, iy, ix, c] + self.sib[iz, iy, ix]
+            return carry
+
+        lax.fori_loop(0, g.Z * g.Y * g.X, add, 0)
+        a, b = self.a, self.b
+        for k in range(1, g.Y):
+            to = (y + k) % g.Y
+            self.copy("a1", self.part.at[:, to, :, c, a[0], a[1]], self.r1a.at[k - 1], g.dev(z, to, x, c))
+        for k in range(1, g.X):
+            to = (x + k) % g.X
+            self.copy("b1", self.part.at[:, :, to, c, b[0], b[1]], self.r1b.at[k - 1], g.dev(z, y, to, c))
+
+    def s2(self):
+        g = self.g
+        z, y, x, c = g.here()
+        self.wait("a1")
+        self.wait("b1")
+        a, b = self.a, self.b
+
+        def add_a(i, carry):
+            iz, ix = i // g.X, i % g.X
+            v = self.part[iz, y, ix, c, a[0], a[1]].astype(jnp.float32)
+            for k in range(g.Y - 1):
+                v = v + self.r1a[k, iz, ix].astype(jnp.float32)
+            self.part[iz, y, ix, c, a[0], a[1]] = v.astype(jnp.bfloat16)
+            return carry
+
+        lax.fori_loop(0, g.Z * g.X, add_a, 0)
+        for k in range(1, g.X):
+            to = (x + k) % g.X
+            self.copy("a2", self.part.at[:, y, to, c, a[0], a[1]], self.r2a.at[k - 1], g.dev(z, y, to, c))
+
+        def add_b(i, carry):
+            iz, iy = i // g.Y, i % g.Y
+            v = self.part[iz, iy, x, c, b[0], b[1]].astype(jnp.float32)
+            for k in range(g.X - 1):
+                v = v + self.r1b[k, iz, iy].astype(jnp.float32)
+            self.part[iz, iy, x, c, b[0], b[1]] = v.astype(jnp.bfloat16)
+            return carry
+
+        lax.fori_loop(0, g.Z * g.Y, add_b, 0)
+        for k in range(1, g.Y):
+            to = (y + k) % g.Y
+            self.copy("b2", self.part.at[:, to, x, c, b[0], b[1]], self.r2b.at[k - 1], g.dev(z, to, x, c))
+
+    def s3(self):
+        g = self.g
+        z, y, x, c = g.here()
+        self.wait("a2")
+        self.wait("b2")
+
+        def add(iz, carry):
+            for h, buf, n in ((self.a, self.r2a, g.X - 1), (self.b, self.r2b, g.Y - 1)):
+                v = self.part[iz, y, x, c, h[0], h[1]].astype(jnp.float32)
+                for k in range(n):
+                    v = v + buf[k, iz].astype(jnp.float32)
+                self.part[iz, y, x, c, h[0], h[1]] = v.astype(jnp.bfloat16)
+            return carry
+
+        lax.fori_loop(0, g.Z, add, 0)
+        for k in range(1, g.Z):
+            to = (z + k) % g.Z
+            self.copy("z", self.part.at[to, y, x, c], self.r3.at[k - 1], g.dev(to, y, x, c))
+
+    def s4(self):
+        g = self.g
+        z, y, x, c = g.here()
+        self.wait("z")
+        v = self.part[z, y, x, c].astype(jnp.float32)
+        for k in range(g.Z - 1):
+            v = v + self.r3[k].astype(jnp.float32)
+        self.out[...] = v
+
+
+def scatter_buffers(g, N, C, cut):
+    r = N // (g.Z * g.F)
+    ha, hb = half_shapes(r, C, cut)
+    return [
+        pltpu.VMEM((g.Z, g.Y, g.X, r, C), jnp.bfloat16),
+        pltpu.VMEM((g.Y - 1, g.Z, g.X, *ha), jnp.bfloat16),
+        pltpu.VMEM((g.X - 1, g.Z, g.Y, *hb), jnp.bfloat16),
+        pltpu.VMEM((g.X - 1, g.Z, *ha), jnp.bfloat16),
+        pltpu.VMEM((g.Y - 1, g.Z, *hb), jnp.bfloat16),
+        pltpu.VMEM((g.Z - 1, r, C), jnp.bfloat16),
+    ]
+
+
+def scatter_kernel(g, cuts, *refs):
+    n = len(cuts)
+    parts, outs = refs[:n], refs[n : 2 * n]
+    bufs = refs[2 * n : 2 * n + 6 * n]
+    send, recv = refs[2 * n + 6 * n :]
+    barrier(g)
+    ts = [
+        Scatter(g, parts[i], outs[i], cuts[i], bufs[6 * i : 6 * i + 6], send.at[i], recv.at[i])
+        for i in range(n)
+    ]
+    for t in ts:
+        t.s0()
+    for tick in range(n + 3):
+        for stage in range(4):
+            i = tick - stage
+            if 0 <= i < n:
+                (ts[i].s1, ts[i].s2, ts[i].s3, ts[i].s4)[stage]()
+    for t in ts:
+        t.finish()
+
+
+def scatter_all(g, parts, cuts):
+    n = len(parts)
+    outs = tuple(jax.ShapeDtypeStruct((p.shape[0] // (g.Z * g.F), p.shape[1]), jnp.float32) for p in parts)
+    count = 1 + 2 * (g.X - 1 + g.Y - 1) + g.Z - 1
+    bufs = []
+    for p, cut in zip(parts, cuts):
+        bufs += scatter_buffers(g, p.shape[0], p.shape[1], cut)
+    return pl.pallas_call(
+        functools.partial(scatter_kernel, g, cuts),
+        out_shape=outs,
+        in_specs=[pl.BlockSpec(memory_space=pltpu.VMEM)] * n,
+        out_specs=tuple([pl.BlockSpec(memory_space=pltpu.VMEM)] * n),
+        scratch_shapes=bufs + [pltpu.SemaphoreType.DMA((n, count)), pltpu.SemaphoreType.DMA((n, count))],
+        compiler_params=pltpu.CompilerParams(
+            collective_id=1, has_side_effects=True, vmem_limit_bytes=60 * 2**20
+        ),
+        name="scatter_gradients",
+    )(*[p.reshape(g.Z, g.Y, g.X, 2, p.shape[0] // (g.Z * g.F), p.shape[1]) for p in parts])
+
+
+GATHER_CUTS = [("row", 8), ("row", 128), ("lane", 256), ("lane", 384), ("lane", 384), ("lane", 384), ("lane", 384)]
+SCATTER_CUTS = [("lane", 384), ("lane", 384), ("lane", 384), ("lane", 384), ("lane", 256), ("row", 128)]
+
+
+def ring_local(
+    g,
+    embed_table,
+    token_ids,
+    time_steps,
+    segment_ids,
+    noise_draw,
+    w_up,
+    w_time,
+    w_qkv,
+    w_out,
+    w_in,
+    w_down,
+    gain_one,
+    gain_two,
+    cotangent,
+):
+    bf = jnp.bfloat16
+    table_values = embed_table.astype(jnp.float32)
+    norm_values = jnp.sqrt(jnp.sum(table_values * table_values, axis=1) + 1e-06)
+    norm_part = jnp.broadcast_to(jnp.sum(norm_values), (16, 128))
+    rows = w_up.shape[1]
+    gains = jnp.stack([gain_one, gain_two], axis=1)
+    gains = jnp.concatenate([gains, jnp.zeros((rows, EMBED - 2), bf)], axis=1)
+    small = jnp.concatenate([w_up.T, w_time.T, gains], axis=1)
+    shards = (norm_part, embed_table, small, w_qkv.T, w_out.T, w_in.T, w_down)
+    norms, full_table, small_full, qkv_t, out_t, in_t, down_full = gather_all(g, shards, GATHER_CUTS, pl.ANY)
+    norm_total = jnp.sum(norms[::16, 0])
+    factor = math.sqrt(EMBED) / (norm_total / VOCAB)
+    embed_t = small_full[:, : 2 * EMBED]
+    gain_first = small_full[:, 2 * EMBED].astype(jnp.float32)
+    gain_second = small_full[:, 2 * EMBED + 1].astype(jnp.float32)
+
+    raw_rows = jnp.take(full_table, token_ids, axis=0).astype(jnp.float32)
+    level_value = time_steps.astype(jnp.float32) / STEPS + 0.0001
+    signal = jnp.sqrt(1.0 - jnp.sqrt(level_value))
+    blur_level = jnp.sqrt(jnp.sqrt(level_value))
+    noisy_input = (
+        signal[:, None] * (raw_rows * factor) + blur_level[:, None] * noise_draw.astype(jnp.float32)
+    ).astype(bf)
+    time_feats = time_features(time_steps).astype(bf)
+    features = jnp.concatenate([noisy_input, time_feats], axis=1)
+    embedded = matmul_right(features, embed_t)
+    normed = layer_norm(embedded, gain_first).astype(bf)
+    mixed_qkv = matmul_right(normed, qkv_t)
+    width = mixed_qkv.shape[1] // 3
+    query_part = mixed_qkv[:, :width].astype(bf)
+    key_part = mixed_qkv[:, width : 2 * width].astype(bf)
+    value_part = mixed_qkv[:, 2 * width :].astype(bf)
+    context, log_total = attention_forward(query_part, key_part, value_part, segment_ids)
+    middle = embedded + matmul_right(context, out_t)
+    normed_two = layer_norm(middle, gain_second).astype(bf)
+    pre_act = matmul_right(normed_two, in_t)
+    activated = gelu_exact(pre_act).astype(bf)
+    output = (middle + matmul(activated, down_full)).astype(bf)
+
+    grad_down = matmul_left(activated, cotangent).astype(bf)
+    grad_act = matmul_right(cotangent, down_full)
+    unused_gelu, gelu_pull = jax.vjp(gelu_exact, pre_act)
+    grad_pre = gelu_pull(grad_act)[0].astype(bf)
+    grad_in = matmul_left(grad_pre, normed_two).astype(bf)
+    grad_normed_two = matmul(grad_pre, in_t)
+    unused_second, second_pull = jax.vjp(layer_norm, middle, gain_second)
+    grad_middle_norm, grad_gain_two = second_pull(grad_normed_two)
+    grad_middle = cotangent.astype(jnp.float32) + grad_middle_norm
+    grad_branch = grad_middle.astype(bf)
+    grad_out = matmul_left(grad_branch, context).astype(bf)
+    grad_context = matmul(grad_branch, out_t).astype(bf)
+    grad_query, grad_key, grad_value = attention_backward(
+        query_part, key_part, value_part, segment_ids, log_total, grad_context
+    )
+    grad_mixed = jnp.concatenate([grad_query, grad_key, grad_value], axis=1)
+    grad_qkv = matmul_left(grad_mixed, normed).astype(bf)
+    grad_normed = matmul(grad_mixed, qkv_t)
+    unused_first, first_pull = jax.vjp(layer_norm, embedded, gain_first)
+    grad_embed_norm, grad_gain_one = first_pull(grad_normed)
+    grad_embedded = (grad_middle + grad_embed_norm).astype(bf)
+    grad_embed_t = matmul_left(grad_embedded, features)
+    grad_noisy = matmul(grad_embedded, embed_t[:, :EMBED])
+    noise_grad = blur_level[:, None] * grad_noisy
+    grad_rows = signal[:, None] * grad_noisy
+    counted = jnp.zeros((VOCAB, EMBED), jnp.float32).at[token_ids].add(grad_rows).astype(bf)
+    grad_gains = jnp.stack([grad_gain_one, grad_gain_two], axis=1)
+    grad_gains = jnp.concatenate([grad_gains, jnp.zeros((grad_gains.shape[0], EMBED - 2), jnp.float32)], axis=1)
+    grad_small = jnp.concatenate([grad_embed_t, grad_gains], axis=1).astype(bf)
+    down_own, in_own, out_own, qkv_own, small_own, counted_own = scatter_all(
+        g, (grad_down, grad_in, grad_out, grad_qkv, grad_small, counted), SCATTER_CUTS
+    )
+    return (
+        output,
+        factor * counted_own,
+        noise_grad,
+        small_own[:, :EMBED].T,
+        small_own[:, EMBED : 2 * EMBED].T,
+        qkv_own.T,
+        out_own.T,
+        in_own.T,
+        down_own,
+        small_own[:, 2 * EMBED],
+        small_own[:, 2 * EMBED + 1],
+    )
+
+
 def solution(mesh):
     in_specs = (
         P(("dp", "fsdp"), None),
@@ -263,4 +688,11 @@
         P(("dp", "fsdp")),
         P(("dp", "fsdp")),
     )
+    grid = Grid(mesh.shape["dp"], mesh.shape["fsdp"])
+
+    def local(*args):
+        if all(rows % 8 == 0 for rows in (args[5].shape[1], args[10].shape[0])):
+            return ring_local(grid, *args)
+        return native_local(*args)
+
     return jax.shard_map(local, mesh=mesh, in_specs=in_specs, out_specs=out_specs, check_vma=False)

time: 1250 us -> 359 us (0.29)
  waiting for transfers between devices: 868 us -> 0 us
  blocking collectives: 202 us -> 0 us
  Pallas kernels: 0 us -> 199 us
  matrix products: 108 us -> 88.5 us
  between operations: 15.8 us -> 2.41 us
    reduce_scatter x5 -> x0, waiting for transfers between devices: 569 us -> none  [the longest x1 142 us: local(): lax.psum_scatter(grad_in, ('dp', 'fsdp'), scatter_dimension=1, tiled=True)]
    pallas_call x0 -> x2, Pallas kernels: none -> 199 us  [the longest x1 104 us: scatter_all(): pl.pallas_call(functools.partial(scatter_kernel, g, cuts), out_shape=outs...]
    unnamed x14 -> x0, waiting for transfers between devices: 199 us -> none
    all_gather x5 -> x0, waiting for transfers between devices: 99.9 us -> none  [the longest x1 57.3 us: local(): lax.all_gather(w_down, ('dp', 'fsdp'), axis=0, tiled=True)]
    unnamed x2 -> x0, blocking collectives: 79.9 us -> none
    all_gather x2 -> x0, blocking collectives: 79.4 us -> none  [the longest x1 41.9 us: local(): lax.all_gather(w_up, ('dp', 'fsdp'), axis=1, tiled=True)]
    psum x1 -> x0, blocking collectives: 42.3 us -> none  [local(): norm_total = lax.psum(jnp.sum(norm_values), ('dp', 'fsdp'))]
    dot_general x6 -> x5, matrix products: 28.8 us -> 15.5 us  [matmul_left(): lax.dot_general(left, right, (((0,), (0,)), ((), ())), preferred_element_...]
  transfers between devices with their start and end apart: 12 -> 0, of which waited for: 9 -> 0; matrix products, arithmetic and copies ran while one was open for 7% -> 0% of each run, Pallas kernels for 0% -> 0%
where the time goes in v1:
time: 359 us; the launch traced here: 355 us
  Pallas kernels  199 us (55%)
  matrix products  88.5 us (25%)
  local copies, waits for them, and re-layouts  33 us (9%)
  other arithmetic  32.4 us (9%)
    pallas_call x1, Pallas kernels, scatter_all(): pl.pallas_call(functools.partial(scatter_kernel, g, cuts), out_shape=outs...  104 us
    pallas_call x1, Pallas kernels, gather_all(): pl.pallas_call(functools.partial(ag_kernel, g, cuts), out_shape=outs, in_...  95.1 us
    dot_general x5, matrix products, matmul_right(): lax.dot_general(left, right, (((1,), (1,)), ((), ())), preferred_element_...  34.7 us
    dot_general x5, matrix products, matmul_left(): lax.dot_general(left, right, (((0,), (0,)), ((), ())), preferred_element_...  15.5 us
    dot_general x5, matrix products, matmul(): return jnp.dot(left, right, preferred_element_type=jnp.float32)  13.7 us
    unnamed x86, local copies, waits for them, and re-layouts  10.1 us
    dot_general x1, matrix products, attention_backward(): jnp.einsum('hqk,qhd->khd', probs_low, g_heads, preferred_element_type=jnp...  8.98 us
    convert_element_type x1, other arithmetic, attention_backward(): grad_scores = grad_scores.astype(jnp.bfloat16)  7.31 us

profile of v1, /device:TPU:0, one launch (start us, length us, event | category | flops | bytes accessed | tf_op | source)
XLA Modules:
  0.0 355.4 jit_solution(10698023587624446119)
XLA Ops:
  2.0 1.0 multiply_reduce_fusion.7
  7.1 1.4 concatenate.23.refs_2_
  8.5 1.2 broadcast_in_dim.45.refs_0_
  10.6 1.0 broadcast_compare_fusion
  11.6 95.1 %gather_weights.1 = (f32[4,2,2,2,16,128]{5,4,3,2,1,0:T(8,128)}, bf16[4,2,2,2,256,128]{5,4,3,2,1,0:T(8,128)(2,1)}, bf16[4,2,2,2,24,384]{5,4,3,2,1,0:T(8,128)(2,1)...) custom-call(f32[16,128]{1,0:T(8,128)} %broadcast_in_dim.45.refs_0_, ...), custom_call_target="tpu_custom_call" | custom-call | tf_op jit(solution)/shard_map/gather_weights/pallas_call | solution.py:361
  106.6 3.4 gather_fusion
  110.0 1.0 slice.40
  112.3 1.2 add_convert_fusion.2
  113.5 1.2 fusion.52
  115.0 1.5 fusion.53
  116.9 4.1 %convolution_convert_fusion.3 = bf16[512,2304]{1,0:T(8,128)(2,1)S(1)} fusion(bf16[2304,768]{1,0:T(8,128)(2,1)} %bitcast.139, f32[512,768]{1,0:T(8,128)S(1)} %get-tuple-element.61, f32[768]{0:T(1024)S(1)} %convert_reduce_fusion.1, f32[512]{0:T(512)S(1)} %fusion.36, f32[512]{0:T(512)S(1)} %broadcast_multiply_fusion.3), kind=kOutput, calls=%fused_computation.41 | convolution fusion | flops 1814691840 | bytes 7478272 | tf_op jit(solution)/shard_map/dot_general | solution.py:36
  121.0 1.3 fusion.51
  122.6 1.7 copy.61
  124.3 2.6 copy.60
  126.9 2.1 fusion.19
  129.0 2.6 fusion
  131.6 1.9 copy-done
  133.6 3.6 %fusion.25 = bf16[12,64,512]{2,1,0:T(8,128)(2,1)S(1)} fusion(bf16[512,12,64]{0,2,1:T(8,128)(2,1)S(1)} %bitcast.102, f32[12,512]{1,0:T(8,128)S(1)} %fusion, f32[12,512]{1,0:T(8,128)S(1)} %get-tuple-element.62, f32[12,512,512]{1,2,0:T(8,128)S(1)} %get-tuple-element.63, pred[512,512]{0,1:T(8,128)(4,1)S(1)} %broadcast_compare_fusion), kind=kOutput, calls=%fused_computation.65 | convolution fusion | flops 418775040 | bytes 14467072 | tf_op jit(solution)/shard_map/hqk,khd->qhd/dot_general | solution.py:70
  138.5 19.9 %multiply_convert_fusion.1 = (bf16[512,3072]{1,0:T(8,128)(2,1)S(1)}, f32[512,3072]{1,0:T(8,128)}, f32[512,3072]{1,0:T(8,128)}) fusion(bf16[3072,768]{1,0:T(8,128)(2,1)} %bitcast.131, f32[512,768]{1,0:T(8,128)S(1)} %get-tuple-element.65, f32[768]{0:T(1024)S(1)} %convert_reduce_fusion, f32[512]{0:T(512)S(1)} %fusion.37, f32[512]{0:T(512)S(1)} %broadcast_multiply_fusion.2), kind=kOutput, calls=%fused_computation.23 | convolution fusion | flops 2519728128 | bytes 22027264 | tf_op jit(solution)/shard_map/dot_general | solution.py:36
  158.4 8.3 %fusion.10 = bf16[512,3072]{1,0:T(8,128)(2,1)S(1)} fusion(f32[512,3072]{1,0:T(8,128)} %get-tuple-element.48, f32[512,3072]{1,0:T(8,128)} %get-tuple-element.66, bf16[3072,768]{1,0:T(8,128)(2,1)S(1)} %bitcast.137, bf16[512,768]{1,0:T(8,128)(2,1)S(1)} %copy-done.8), kind=kOutput, calls=%fused_computation.20 | convolution fusion | flops 2437939200 | bytes 21233664 | tf_op jit(solution)/shard_map/dot_general | solution.py:36
  166.7 3.5 add_convert_fusion.1
  170.2 2.8 multiply_reduce_fusion.1
  173.7 4.7 %convolution_convert_fusion.1 = bf16[3072,768]{1,0:T(8,128)(2,1)} fusion(bf16[512,3072]{1,0:T(8,128)(2,1)S(1)} %fusion.10, f32[512,768]{1,0:T(8,128)S(1)} %get-tuple-element.65, f32[768]{0:T(1024)S(1)} %convert_reduce_fusion, f32[512]{0:T(512)S(1)} %fusion.37, f32[512]{0:T(512)S(1)} %broadcast_multiply_fusion.2), kind=kOutput, calls=%fused_computation.39 | convolution fusion | flops 2419851264 | bytes 9444352 | tf_op jit(solution)/shard_map/dot_general | solution.py:30
  178.4 1.0 concatenate.31
  179.5 1.5 fusion.26
  180.9 3.0 convolution_convert_fusion.5
  183.9 1.9 convolution_convert_fusion.4
  185.8 2.3 copy.66
  188.1 9.0 %fusion.22 = bf16[12,64,512]{2,1,0:T(8,128)(2,1)} fusion(bf16[512,12,64]{0,2,1:T(8,128)(2,1)} %bitcast.104, f32[12,512]{1,0:T(8,128)S(1)} %log_add_fusion, f32[12,512,512]{1,2,0:T(8,128)} %copy-done, pred[512,512]{0,1:T(8,128)(4,1)S(1)} %broadcast_compare_fusion), kind=kOutput, calls=%fused_computation.64 | convolution fusion | flops 415629312 | bytes 14442496 | tf_op jit(solution)/shard_map/hqk,qhd->khd/dot_general | solution.py:87
  197.1 4.4 %convolution_convert_fusion.2 = bf16[3072,768]{1,0:T(8,128)(2,1)} fusion(bf16[512,3072]{1,0:T(8,128)(2,1)S(1)} %copy-done.32, bf16[512,768]{1,0:T(8,128)(2,1)S(1)} %copy-done.9), kind=kOutput, calls=%fused_computation.40 | convolution fusion | flops 2418278400 | bytes 8650752 | tf_op jit(solution)/shard_map/dot_general | solution.py:30
  201.5 6.9 %multiply_reduce_fusion = (f32[12,512]{1,0:T(8,128)S(1)}, f32[12,512,512]{1,2,0:T(8,128)}) fusion(f32[12,512]{1,0:T(8,128)S(1)} %log_add_fusion, f32[12,512,512]{1,2,0:T(8,128)S(1)} %bitcast.93, pred[512,512]{0,1:T(8,128)(4,1)S(1)} %broadcast_compare_fusion, bf16[512,12,64]{0,2,1:T(8,128)(2,1)S(1)} %bitcast.105, bf16[512,12,64]{0,2,1:T(8,128)(2,1)S(1)} %bitcast.103), kind=kOutput, calls=%fused_computation.3 | convolution fusion | flops 418375680 | bytes 27049984 | tf_op jit(solution)/shard_map/qhd,khd->hqk/dot_general | solution.py:86
  208.4 7.3 %multiply_convert_fusion = bf16[12,512,512]{1,2,0:T(8,128)(2,1)S(1)} fusion(f32[12,512,512]{1,2,0:T(8,128)} %get-tuple-element.69, f32[12,512]{1,0:T(8,128)S(1)} %get-tuple-element.68, f32[12,512]{1,0:T(8,128)S(1)} %log_add_fusion, f32[12,512,512]{1,2,0:T(8,128)S(1)} %bitcast.93, pred[512,512]{0,1:T(8,128)(4,1)S(1)} %broadcast_compare_fusion), kind=kLoop, calls=%fused_computation.2 | loop fusion | flops 18874368 | bytes 31768576 | tf_op jit(solution)/shard_map/convert_element_type | solution.py:91
  215.7 2.0 multiply_convert_fusion.2
  217.7 1.1 multiply_convert_fusion.3
  219.9 2.4 multiply_reduce_fusion.3
  223.0 4.0 %convolution_convert_fusion = bf16[2304,768]{1,0:T(8,128)(2,1)} fusion(bf16[512,768]{0,1:T(8,128)(2,1)S(1)} %bitcast.142, bf16[512,768]{0,1:T(8,128)(2,1)S(1)} %bitcast.117, bf16[512,768]{0,1:T(8,128)(2,1)S(1)} %bitcast.107, f32[512,768]{1,0:T(8,128)S(1)} %get-tuple-element.61, f32[768]{0:T(1024)S(1)} %convert_reduce_fusion.1, f32[512]{0:T(512)S(1)} %fusion.36, ...), kind=kOutput, calls=%fused_computation.38 | convolution fusion | flops 1822359552 | bytes 7478272 | tf_op jit(solution)/shard_map/dot_general | solution.py:30
  227.7 2.0 broadcast_multiply_fusion
  230.6 1.0 maximum_maximum_fusion.refs_4_
  231.6 4.7 %scatter_custom_fusion = f32[8192,128]{1,0:T(8,128)} fusion(s32[512]{0:T(512)} %copy-done.27, f32[]{:T(128)} %constant.54.clone.1, f32[512,128]{1,0:T(8,128)S(1)} %get-tuple-element.72, f32[512]{0:T(512)S(1)} %copy-done.22), kind=kCustom, calls=%fused_computation.46 | custom fusion | flops 131072 | bytes 4459008 | tf_op jit(solution)/shard_map/scatter-add | solution.py:639
  236.2 3.8 %convert_element_type.168 = bf16[8192,128]{1,0:T(8,128)(2,1)} convert(f32[8192,128]{1,0:T(8,128)} %scatter_custom_fusion) | non-fusion elementwise | flops 1048576 | bytes 6291456 | tf_op jit(solution)/shard_map/convert_element_type | solution.py:639
  240.0 104.0 %scatter_gradients.1 = (f32[96,768]{1,0:T(8,128)}, f32[96,768]{1,0:T(8,128)}, f32[24,768]{1,0:T(8,128)}, f32[72,768]{1,0:T(8,128)}, f32[24,384]{1,0:T(8,128)}, /*index=5*/f32[256,128]{1,0:T(8,128)}) custom-call(bf16[4,2,2,2,96,768]{5,4,3,2,1,0:T(8,128)(2,1)} %bitcast.100, bf16[4,2,2,2,96,768]{5,4,3,2,1,0:T(8,128)(2,1)} %bitcast.99, ...), custom_call_target="tpu_custom_call" | custom-call | tf_op jit(solution)/shard_map/scatter_gradients/pallas_call | solution.py:541
  344.0 1.6 broadcast_multiply_fusion.1
  345.6 1.5 slice_reduce_fusion
  347.1 1.3 slice_bitcast_fusion
  348.4 1.6 copy.83
  350.1 1.5 copy.84
  351.6 1.7 copy.85
  353.3 1.7 copy.86
  (120 shorter events, 13.0 us)
Async XLA Ops:
  4.2 1.4 copy-start.27
  5.6 106.7 %copy-start.21 = (f32[512]{0:T(512)}, f32[512]{0:T(512)S(1)}, u32[]{:S(2)}) copy-start(f32[512]{0:T(512)S(1)} %get-tuple-element.58) | copy-start | bytes 6148
  5.6 106.7 %copy-start.23 = (f32[512]{0:T(512)}, f32[512]{0:T(512)S(1)}, u32[]{:S(2)}) copy-start(f32[512]{0:T(512)S(1)} %get-tuple-element.59) | copy-start | bytes 6148
  10.5 110.5 %copy-start.17 = (bf16[512,64]{1,0:T(8,128)(2,1)}, bf16[512,64]{1,0:T(8,128)(2,1)S(1)}, u32[]{:S(2)}) copy-start(bf16[512,64]{1,0:T(8,128)(2,1)S(1)} %copy.57) | copy-start | bytes 196612
  10.6 110.4 %copy-start.19 = (bf16[512,64]{1,0:T(8,128)(2,1)}, bf16[512,64]{1,0:T(8,128)(2,1)S(1)}, u32[]{:S(2)}) copy-start(bf16[512,64]{1,0:T(8,128)(2,1)S(1)} %copy.58) | copy-start | bytes 196612
  113.5 7.5 %copy-start.15 = (bf16[512,128]{1,0:T(8,128)(2,1)}, bf16[512,128]{1,0:T(8,128)(2,1)S(1)}, u32[]{:S(2)}) copy-start(bf16[512,128]{1,0:T(8,128)(2,1)S(1)} %add_convert_fusion.2) | copy-start | bytes 393220
  116.8 4.2 %copy-start.25 = (f32[512]{0:T(512)}, f32[512]{0:T(512)S(1)}, u32[]{:S(2)}) copy-start(f32[512]{0:T(512)S(1)} %multiply_reduce_fusion.6) | copy-start | bytes 6148
  122.6 6.4 %copy-start.1 = (bf16[512,768]{0,1:T(8,128)(2,1)}, bf16[512,768]{0,1:T(8,128)(2,1)S(1)}, u32[]{:S(2)}) copy-start(bf16[512,768]{0,1:T(8,128)(2,1)S(1)} %copy.62) | copy-start | bytes 2359300
  124.3 4.7 %copy-start.3 = (bf16[512,768]{0,1:T(8,128)(2,1)}, bf16[512,768]{0,1:T(8,128)(2,1)S(1)}, u32[]{:S(2)}) copy-start(bf16[512,768]{0,1:T(8,128)(2,1)S(1)} %copy.61) | copy-start | bytes 2359300
  129.0 4.6 %copy-start = (f32[12,512,512]{1,2,0:T(8,128)}, f32[12,512,512]{1,2,0:T(8,128)S(1)}, u32[]{:S(2)}) copy-start(f32[12,512,512]{1,2,0:T(8,128)S(1)} %get-tuple-element.63) | copy-start | bytes 37748740
  129.0 4.5 %copy-start.5 = (bf16[512,768]{0,1:T(8,128)(2,1)S(1)}, bf16[512,768]{0,1:T(8,128)(2,1)}, u32[]{:S(2)}) copy-start(bf16[512,768]{0,1:T(8,128)(2,1)} %copy.60) | copy-start | bytes 2359300
  133.6 3.6 %copy-start.11 = (bf16[4,2,2,2,24,768]{5,4,3,2,1,0:T(8,128)(2,1)S(1)}, bf16[4,2,2,2,24,768]{5,4,3,2,1,0:T(8,128)(2,1)}, u32[]{:S(2)}) copy-start(bf16[4,2,2,2,24,768]{5,4,3,2,1,0:T(8,128)(2,1)} %get-tuple-element.28) | copy-start | bytes 3538948
  137.2 21.2 %copy-start.12 = (bf16[12,64,512]{2,1,0:T(8,128)(2,1)}, bf16[12,64,512]{2,1,0:T(8,128)(2,1)S(1)}, u32[]{:S(2)}) copy-start(bf16[12,64,512]{2,1,0:T(8,128)(2,1)S(1)} %fusion.25) | copy-start | bytes 2359300
  137.2 21.2 %slice-start.5 = ((s8[4718592]{0:T(1024)(128)(4,1)}), s8[4194304]{0:T(1024)(128)(4,1)S(1)}, s32[]{:S(2)}) async-start(s8[4718592]{0:T(1024)(128)(4,1)} %bitcast.135), calls=%async_computation.5 | async-start | bytes 8388608
  137.2 33.0 %slice-start.3 = ((s8[4718592]{0:T(1024)(128)(4,1)}), s8[4194304]{0:T(1024)(128)(4,1)S(1)}, s32[]{:S(2)}) async-start(s8[4718592]{0:T(1024)(128)(4,1)} %bitcast.132), calls=%async_computation.3 | async-start | bytes 8388608
  138.4 19.9 %copy-start.8 = (bf16[512,768]{1,0:T(8,128)(2,1)S(1)}, bf16[512,768]{1,0:T(8,128)(2,1)}, u32[]{:S(2)}) copy-start(bf16[512,768]{1,0:T(8,128)(2,1)} %param.27) | copy-start | bytes 2359300
  138.5 19.9 %slice-start.6 = ((s8[4718592]{0:T(1024)(128)(4,1)}), s8[524288]{0:T(1024)(128)(4,1)S(1)}, s32[]{:S(2)}) async-start(s8[4718592]{0:T(1024)(128)(4,1)} %bitcast.135), calls=%async_computation.6 | async-start | bytes 1048576
  138.5 31.7 %slice-start.4 = ((s8[4718592]{0:T(1024)(128)(4,1)}), s8[524288]{0:T(1024)(128)(4,1)S(1)}, s32[]{:S(2)}) async-start(s8[4718592]{0:T(1024)(128)(4,1)} %bitcast.132), calls=%async_computation.4 | async-start | bytes 1048576
  158.3 8.3 %copy-start.31 = (bf16[512,3072]{1,0:T(8,128)(2,1)}, bf16[512,3072]{1,0:T(8,128)(2,1)S(1)}, u32[]{:S(2)}) copy-start(bf16[512,3072]{1,0:T(8,128)(2,1)S(1)} %get-tuple-element.47) | copy-start | bytes 9437188
  179.5 4.4 %copy-start.13 = (bf16[12,64,512]{2,1,0:T(8,128)(2,1)S(1)}, bf16[12,64,512]{2,1,0:T(8,128)(2,1)}, u32[]{:S(2)}) copy-start(bf16[12,64,512]{2,1,0:T(8,128)(2,1)} %copy-done.12) | copy-start | bytes 2359300
  188.1 9.0 %copy-start.9 = (bf16[512,768]{1,0:T(8,128)(2,1)S(1)}, bf16[512,768]{1,0:T(8,128)(2,1)}, u32[]{:S(2)}) copy-start(bf16[512,768]{1,0:T(8,128)(2,1)} %param.27) | copy-start | bytes 2359300
  188.1 9.0 %copy-start.32 = (bf16[512,3072]{1,0:T(8,128)(2,1)S(1)}, bf16[512,3072]{1,0:T(8,128)(2,1)}, u32[]{:S(2)}) copy-start(bf16[512,3072]{1,0:T(8,128)(2,1)} %copy-done.31) | copy-start | bytes 9437188
  188.1 13.4 %slice-start = ((s8[12582912]{0:T(1024)(128)(4,1)}), s8[4194304]{0:T(1024)(128)(4,1)S(1)}, s32[]{:S(2)}) async-start(s8[12582912]{0:T(1024)(128)(4,1)} %bitcast.92), calls=%async_computation | async-start | bytes 8388608
  188.1 13.4 %slice-start.1 = ((s8[12582912]{0:T(1024)(128)(4,1)}), s8[4194304]{0:T(1024)(128)(4,1)S(1)}, s32[]{:S(2)}) async-start(s8[12582912]{0:T(1024)(128)(4,1)} %bitcast.92), calls=%async_computation.1 | async-start | bytes 8388608
  197.1 4.4 %slice-start.2 = ((s8[12582912]{0:T(1024)(128)(4,1)}), s8[4194304]{0:T(1024)(128)(4,1)S(1)}, s32[]{:S(2)}) async-start(s8[12582912]{0:T(1024)(128)(4,1)} %bitcast.92), calls=%async_computation.2 | async-start | bytes 8388608
  197.1 4.4 %copy-start.6 = (bf16[512,768]{0,1:T(8,128)(2,1)S(1)}, bf16[512,768]{0,1:T(8,128)(2,1)}, u32[]{:S(2)}) copy-start(bf16[512,768]{0,1:T(8,128)(2,1)} %copy.60) | copy-start | bytes 2359300
  197.1 4.4 %copy-start.7 = (bf16[512,768]{0,1:T(8,128)(2,1)S(1)}, bf16[512,768]{0,1:T(8,128)(2,1)}, u32[]{:S(2)}) copy-start(bf16[512,768]{0,1:T(8,128)(2,1)} %copy.66) | copy-start | bytes 2359300
  208.4 7.3 %copy-start.4 = (bf16[512,768]{0,1:T(8,128)(2,1)S(1)}, bf16[512,768]{0,1:T(8,128)(2,1)}, u32[]{:S(2)}) copy-start(bf16[512,768]{0,1:T(8,128)(2,1)} %copy-done.3) | copy-start | bytes 2359300
  215.7 2.0 copy-start.2
  217.7 2.0 copy-start.29
  217.7 2.2 copy-start.30
  219.9 2.4 copy-start.26
  223.0 4.1 %copy-start.10 = (bf16[512,768]{1,0:T(8,128)(2,1)S(1)}, bf16[512,768]{1,0:T(8,128)(2,1)}, u32[]{:S(2)}) copy-start(bf16[512,768]{1,0:T(8,128)(2,1)} %param.27) | copy-start | bytes 2359300
  227.0 0.7 copy-start.24
  227.0 2.7 copy-start.16
  227.0 2.7 copy-start.18
  227.0 2.7 copy-start.20
  227.0 3.5 copy-start.14
  227.0 3.5 copy-start.28
  227.1 4.5 %copy-start.22 = (f32[512]{0:T(512)S(1)}, f32[512]{0:T(512)}, u32[]{:S(2)}) copy-start(f32[512]{0:T(512)} %copy-done.21) | copy-start | bytes 6148

commit v2 on v0

--- a/solution.py
+++ b/solution.py
@@ -1,8 +1,11 @@
+import functools
 import math
 
 import jax
 import jax.numpy as jnp
 from jax import lax
+from jax.experimental import pallas as pl
+from jax.experimental.pallas import tpu as pltpu
 from jax.sharding import PartitionSpec as P
 
 HEADS = 12
@@ -100,7 +103,7 @@
     return (grad_query, grad_key, grad_value)
 
 
-def local(
+def native_local(
     embed_table,
     token_ids,
     time_steps,
@@ -233,6 +236,767 @@
     )
 
 
+MESH = pl.DeviceIdType.MESH
+
+
+class Grid:
+    def __init__(self, Z, F):
+        self.Z, self.F = Z, F
+        self.X = math.isqrt(F // 2)
+        self.Y = F // 2 // self.X
+        self.size = {"z": self.Z, "y": self.Y, "x": self.X}
+
+    def here(self):
+        f = lax.axis_index("fsdp")
+        return {"z": lax.axis_index("dp"), "y": f // (2 * self.X), "x": (f // 2) % self.X, "c": f % 2}
+
+    def dev(self, at):
+        return (at["z"], (at["y"] * self.X + at["x"]) * 2 + at["c"])
+
+    def moved(self, at, d, k):
+        return {**at, d: (at[d] + k) % self.size[d]}
+
+    def sibling(self, at):
+        return {**at, "c": 1 - at["c"]}
+
+
+def enter(g, at):
+    bar = pltpu.get_barrier_semaphore()
+    peers = [g.moved(at, d, k) for d in "zyx" for k in range(1, g.size[d])] + [g.sibling(at)]
+    for p in peers:
+        pl.semaphore_signal(bar, inc=1, device_id=g.dev(p), device_id_type=MESH)
+    pl.semaphore_wait(bar, len(peers))
+
+
+def halves(r, C, cut):
+    kind, to = cut
+    if kind == "lane":
+        return ((pl.ds(0, r), pl.ds(0, to)), (pl.ds(0, r), pl.ds(to, C - to)))
+    return ((pl.ds(0, to), pl.ds(0, C)), (pl.ds(to, r - to), pl.ds(0, C)))
+
+
+def half_shapes(r, C, cut):
+    kind, to = cut
+    return ((r, to), (r, C - to)) if kind == "lane" else ((to, C), (r - to, C))
+
+
+class Mover:
+    def __init__(self, send, recv):
+        self.send, self.recv, self.count, self.groups = send, recv, 0, {}
+
+    def copy(self, group, src, dst, dev):
+        c = pltpu.make_async_remote_copy(
+            src_ref=src, dst_ref=dst, send_sem=self.send.at[self.count], recv_sem=self.recv.at[self.count],
+            device_id=dev, device_id_type=MESH,
+        )
+        self.count += 1
+        c.start()
+        self.groups.setdefault(group, []).append(c)
+
+    def wait(self, group):
+        for c in self.groups.get(group, []):
+            c.wait_recv()
+
+    def sent(self):
+        for cs in self.groups.values():
+            for c in cs:
+                c.wait_send()
+        self.groups = {}
+
+
+def gather_copies(g):
+    return 2 * (sum(n - 1 for n in g.size.values()) + 1 + sum(n - 1 for n in g.size.values()))
+
+
+class Gather:
+    def __init__(self, g, at, mover, shard, full, cut, orders):
+        self.g, self.at, self.mover, self.shard, self.full = g, at, mover, shard, full
+        self.halves = halves(*shard.shape, cut)
+        self.orders = orders
+        self.rows = shard.shape[0]
+
+    def view(self, h, index):
+        rows, lanes = self.halves[h]
+        return self.full.at[index["z"], index["y"], index["x"], self.at["c"], rows, lanes]
+
+    def own(self, sem):
+        at = self.at
+        rows, lanes = self.halves[0][0], self.halves[0][1]
+        self.local = pltpu.make_async_copy(
+            self.shard, self.full.at[at["z"], at["y"], at["x"], at["c"], pl.ds(0, self.rows)], sem
+        )
+        self.local.start()
+
+    def held(self, h, stage):
+        at = self.at
+        return {d: slice(None) if d in self.orders[h][:stage] else at[d] for d in "zyx"}
+
+    def send(self, stage):
+        g, at = self.g, self.at
+        if stage == 2:
+            self.local.wait()
+        for h in (0, 1):
+            d = self.orders[h][stage - 1]
+            if stage > 1:
+                self.mover.wait((h, stage - 1))
+            for k in range(1, g.size[d]):
+                dst = self.view(h, self.held(h, stage - 1))
+                src = dst if stage > 1 else self.shard.at[self.halves[h]]
+                self.mover.copy((h, stage), src, dst, g.dev(g.moved(at, d, k)))
+        for h in (0, 1):
+            if stage > 1:
+                self.share(h, stage - 1)
+
+    def share(self, h, stage):
+        g, at = self.g, self.at
+        d = self.orders[h][stage - 1]
+        sib = g.dev(g.sibling(at))
+        if stage == 1:
+            v = self.view(h, self.held(h, 1))
+            self.mover.copy("sib", v, v, sib)
+            return
+        for k in range(1, g.size[d]):
+            index = {**self.held(h, stage - 1), d: g.moved(at, d, -k)[d]}
+            v = self.view(h, index)
+            self.mover.copy("sib", v, v, sib)
+
+    def last(self):
+        for h in (0, 1):
+            self.mover.wait((h, 3))
+            self.share(h, 3)
+
+    def done(self):
+        self.mover.wait("sib")
+
+
+class Scatter:
+    def __init__(self, g, at, mover, part, rows, out, cut, orders, bufs):
+        self.g, self.at, self.mover, self.part, self.out, self.rows = g, at, mover, part, out, rows
+        self.halves = halves(rows, part.shape[-1], cut)
+        self.orders = orders
+        self.sib, self.bufs = bufs[0], (bufs[1:4], bufs[4:7])
+
+    def view(self, h, index):
+        rows, lanes = self.halves[h]
+        return self.part.at[index["z"], index["y"], index["x"], self.at["c"], rows, lanes]
+
+    def index(self, h, stage, other=None):
+        at, order = self.at, self.orders[h]
+        index = {d: at[d] if d in order[:stage] else slice(None) for d in "zyx"}
+        if other is not None:
+            index[order[stage - 1]] = other
+        return index
+
+    def start(self):
+        g, at = self.g, self.at
+        src = self.part.at[:, :, :, 1 - at["c"], pl.ds(0, self.rows)]
+        self.mover.copy("sib", src, self.sib, g.dev(g.sibling(at)))
+
+    def send(self, stage):
+        g, at = self.g, self.at
+        if stage == 1:
+            self.mover.wait("sib")
+            rows, c = pl.ds(0, self.rows), at["c"]
+
+            def add(i, carry):
+                iz, iy, ix = i // (g.Y * g.X), (i // g.X) % g.Y, i % g.X
+                self.part[iz, iy, ix, c, rows] = self.part[iz, iy, ix, c, rows] + self.sib[iz, iy, ix]
+                return carry
+
+            lax.fori_loop(0, g.Z * g.Y * g.X, add, 0)
+        for h in (0, 1):
+            if stage > 1:
+                self.add(h, stage - 1)
+            d = self.orders[h][stage - 1]
+            for k in range(1, g.size[d]):
+                to = g.moved(at, d, k)
+                self.mover.copy((h, stage), self.view(h, self.index(h, stage, to[d])), self.bufs[h][stage - 1].at[k - 1], g.dev(to))
+
+    def add(self, h, stage):
+        g = self.g
+        self.mover.wait((h, stage))
+        free = [d for d in "zyx" if d not in self.orders[h][:stage]]
+        sizes = [g.size[d] for d in free]
+        buf = self.bufs[h][stage - 1]
+        rows, lanes = self.halves[h]
+
+        def body(i, carry):
+            index = dict(self.at)
+            place = []
+            for n, d in zip(reversed(sizes), reversed(free)):
+                index[d] = i % n
+                place.insert(0, i % n)
+                i = i // n
+            where = (index["z"], index["y"], index["x"], self.at["c"], rows, lanes)
+            v = self.part[where].astype(jnp.float32)
+            for k in range(buf.shape[0]):
+                v = v + buf[(k, *place)].astype(jnp.float32)
+            self.part[where] = v.astype(self.part.dtype)
+            return carry
+
+        lax.fori_loop(0, math.prod(sizes), body, 0)
+
+    def last(self, sem=None):
+        at = self.at
+        for h in (0, 1):
+            self.mover.wait((h, 3))
+            rows, lanes = self.halves[h]
+            v = self.part[at["z"], at["y"], at["x"], at["c"], rows, lanes].astype(jnp.float32)
+            buf = self.bufs[h][2]
+            for k in range(buf.shape[0]):
+                v = v + buf[k].astype(jnp.float32)
+            self.out[rows, lanes] = v
+
+
+def scatter_copies(g):
+    return 1 + 2 * sum(n - 1 for n in g.size.values())
+
+
+def scatter_buffers(g, r, C, cut, orders, dtype):
+    shapes = [(g.Z, g.Y, g.X, r, C)]
+    for hs, order in zip(half_shapes(r, C, cut), orders):
+        for stage in (1, 2, 3):
+            free = [g.size[d] for d in "zyx" if d not in order[:stage]]
+            shapes.append((g.size[order[stage - 1]] - 1, *free, *hs))
+    return [pltpu.VMEM(s, dtype) for s in shapes]
+
+
+ZXY, XZY = (("z", "x", "y"), ("z", "y", "x")), (("x", "z", "y"), ("y", "z", "x"))
+YXZ, YZX = (("y", "x", "z"), ("x", "y", "z")), (("y", "z", "x"), ("x", "z", "y"))
+
+
+bf16, f32 = jnp.bfloat16, jnp.float32
+
+
+def dot_nn(left, right):
+    return jnp.dot(left, right, preferred_element_type=f32)
+
+
+def dot_nt(left, right):
+    return lax.dot_general(left, right, (((1,), (1,)), ((), ())), preferred_element_type=f32)
+
+
+def dot_tn(left, right):
+    return lax.dot_general(left, right, (((0,), (0,)), ((), ())), preferred_element_type=f32)
+
+
+def block(i, n):
+    return pl.ds(pl.multiple_of(i * n, n), n)
+
+
+def normalize(v):
+    width = v.shape[1]
+    center = v - jnp.sum(v, axis=1, keepdims=True) * (1.0 / width)
+    spread = jnp.sum(center * center, axis=1, keepdims=True) * (1.0 / width)
+    scale = lax.rsqrt(spread + 1e-05)
+    return center * scale, scale
+
+
+def norm_forward(src, gain, dst):
+    def body(i, carry):
+        rows = block(i, 64)
+        n, _ = normalize(src[rows, :])
+        dst[rows, :] = (n * gain).astype(bf16)
+        return carry
+
+    lax.fori_loop(0, src.shape[0] // 64, body, 0)
+
+
+def norm_backward(src, gain, up, put):
+    width = src.shape[1]
+
+    def body(i, total):
+        rows = block(i, 64)
+        n, scale = normalize(src[rows, :])
+        u = up[rows, :]
+        a = u * gain
+        mean_a = jnp.sum(a, axis=1, keepdims=True) * (1.0 / width)
+        mean_an = jnp.sum(a * n, axis=1, keepdims=True) * (1.0 / width)
+        put(rows, scale * (a - mean_a - n * mean_an))
+        return total + jnp.sum((u * n).reshape(8, 8, width), axis=0)
+
+    return lax.fori_loop(0, src.shape[0] // 64, body, jnp.zeros((8, width), f32))
+
+
+def places(g):
+    return [(z, y, x, c) for z in range(g.Z) for y in range(g.Y) for x in range(g.X) for c in (0, 1)]
+
+
+def layer_kernel(g, tensors, *refs):
+    n_in, n_out = 14, 9
+    (table_s, up_s, time_s, qkv_s, out_s, in_s, down_s, one_s, two_s, ids, steps, segs, noise, cot) = refs[:n_in]
+    (output, noise_grad, table_o, small_o, qkv_o, out_o, in_o, down_o, gains_o) = refs[n_in : n_in + n_out]
+    rest = list(refs[n_in + n_out :])
+    take = lambda n: [rest.pop(0) for _ in range(n)]
+    (small_s, gains_s, wtable, wsmall, wgains, wqkv, wout, win, wdown) = take(9)
+    (small_nat, qkv_nat, out_nat, gain_rows, factor_s, level_s) = take(6)
+    (feats, emb, normed, mixed, context, lse, mid, normed_two, act, slope, grad_t, raw, bias) = take(13)
+    bufs = {name: take(7) for name in ("down", "in", "out", "qkv", "small", "gains", "table")}
+    local, ag_send, ag_recv, rs_send, rs_recv = take(5)
+
+    at = g.here()
+    tokens, width = cot.shape
+    rows = up_s.shape[0]
+    heads = width // HEAD_DIM
+    vocab = table_s.shape[0] * g.Z * g.F
+    hidden = in_s.shape[0] * g.Z * g.F
+    groups = tokens // 64
+    spots = places(g)
+
+    small_s[:, :EMBED] = up_s[...]
+    small_s[:, EMBED:] = time_s[...]
+    gains_s[...] = jnp.zeros_like(gains_s)
+    gains_s[0:1, 0:rows] = one_s[...].astype(f32)
+    gains_s[8:9, 0:rows] = two_s[...].astype(f32)
+    tv = table_s[...].astype(f32)
+    norms = jnp.sqrt(jnp.sum(tv * tv, axis=1, keepdims=True) + 1e-06)
+    gains_s[9:10, :] = jnp.broadcast_to(jnp.sum(norms, axis=0, keepdims=True), (1, 128))
+
+    enter(g, at)
+    shards = {"gains": gains_s, "small": small_s, "table": table_s, "qkv": qkv_s, "out": out_s, "in": in_s, "down": down_s}
+    fulls = {"gains": wgains, "small": wsmall, "table": wtable, "qkv": wqkv, "out": wout, "in": win, "down": wdown}
+    ag = {}
+    for i, name in enumerate(shards):
+        cut, orders, _ = tensors[name]
+        ag[name] = Gather(g, at, Mover(ag_send.at[i], ag_recv.at[i]), shards[name], fulls[name], cut, orders)
+        ag[name].own(local.at[i])
+        ag[name].send(1)
+    first = [ag["gains"], ag["small"], ag["table"]]
+
+    is_long = segs[tokens - 1] == 0
+    row_block = lax.broadcasted_iota(jnp.int32, (tokens, tokens), 0) // 64
+    col_block = lax.broadcasted_iota(jnp.int32, (tokens, tokens), 1) // 64
+    bias[...] = jnp.where(row_block == col_block, 0.0, jnp.where(is_long, 0.0, -1e30)).astype(bf16)
+    sub = lax.broadcasted_iota(jnp.int32, (8, 128), 0)
+    lane = lax.broadcasted_iota(jnp.int32, (8, 128), 1)
+    t = jnp.zeros((8, 128), f32)
+    for i in range(groups):
+        t = jnp.where(sub == i, steps[64 * i].astype(f32), t)
+    level = t / STEPS + 0.0001
+    level_s[0:8, :] = jnp.sqrt(1.0 - jnp.sqrt(level))
+    level_s[8:16, :] = jnp.sqrt(jnp.sqrt(level))
+    half = TIME_DIM // 2
+    angles = t * jnp.exp(-math.log(10000.0) * (lane % half).astype(f32) / half)
+    waves = jnp.where(lane < half, jnp.sin(angles), jnp.cos(angles))
+    for i in range(groups):
+        feats[64 * i : 64 * i + 64, EMBED:] = jnp.broadcast_to(waves[i : i + 1], (64, TIME_DIM)).astype(bf16)
+    ids_row = ids[...].astype(f32)
+    ids_col = jnp.transpose(jnp.broadcast_to(ids_row, (128, tokens)))
+
+    for s in first:
+        s.send(2)
+    for s in first:
+        s.send(3)
+    ag["qkv"].send(2)
+    for s in first:
+        s.last()
+    ag["out"].send(2)
+    for s in first:
+        s.done()
+
+    ones = [jnp.zeros((8, 128), f32) for _ in range(width // 128)]
+    twos = [jnp.zeros((8, 128), f32) for _ in range(width // 128)]
+    total = jnp.zeros((8, 128), f32)
+    for d, spot in enumerate(spots):
+        a, b = wgains[(*spot, pl.ds(0, 8))], wgains[(*spot, pl.ds(8, 8))]
+        total = total + b
+        j, shift = (rows * d) // 128, (rows * d) % 128
+        for acc, v in ((ones, a), (twos, b)):
+            v = jnp.where(sub == 0, v, 0.0)
+            r = pltpu.roll(v, shift, axis=1) if shift else v
+            if shift + rows <= 128:
+                acc[j] = acc[j] + r
+            else:
+                acc[j] = acc[j] + jnp.where(lane >= shift, r, 0.0)
+                acc[j + 1] = acc[j + 1] + jnp.where(lane < shift, r, 0.0)
+    for j in range(width // 128):
+        gain_rows[0:8, 128 * j : 128 * j + 128] = ones[j]
+        gain_rows[8:16, 128 * j : 128 * j + 128] = twos[j]
+    factor = math.sqrt(EMBED) / (jnp.broadcast_to(total[1:2, :], (8, 128)) * (1.0 / vocab))
+    factor_s[...] = factor
+    for d, spot in enumerate(spots):
+        small_nat[rows * d : rows * d + rows, :] = wsmall[spot]
+
+    table = wtable.reshape(vocab, EMBED)
+    span = 1024
+    raw[...] = jnp.zeros_like(raw)
+
+    def pick(i, carry):
+        base = (i * span).astype(f32)
+        cells = [
+            jnp.where(ids_col == (lax.broadcasted_iota(jnp.int32, (tokens, 128), 1) + 128 * b).astype(f32) + base, 1.0, 0.0).astype(bf16)
+            for b in range(span // 128)
+        ]
+        raw[...] += dot_nn(jnp.concatenate(cells, axis=1), table[block(i, span), :])
+        return carry
+
+    lax.fori_loop(0, vocab // span, pick, 0)
+    ag["qkv"].send(3)
+    for i in range(groups):
+        r = slice(64 * i, 64 * i + 64)
+        signal, blur = level_s[i : i + 1, :], level_s[8 + i : 9 + i, :]
+        feats[r, :EMBED] = (signal * (raw[r, :] * factor_s[0:1, :]) + blur * noise[r, :].astype(f32)).astype(bf16)
+    emb[...] = dot_nt(feats[...], small_nat[...])
+    norm_forward(emb, gain_rows[0:1, :], normed)
+    ag["out"].send(3)
+    ag["in"].send(2)
+    ag["qkv"].last()
+    ag["qkv"].done()
+
+    for d, spot in enumerate(spots):
+        qkv_nat[3 * rows * d : 3 * rows * (d + 1), :] = wqkv[(*spot, pl.ds(0, 3 * rows))]
+
+    def project(j, carry):
+        mixed[:, block(j, width)] = dot_nt(normed[...], qkv_nat[block(j, width), :]).astype(bf16)
+        return carry
+
+    lax.fori_loop(0, 3, project, 0)
+    ag["out"].last()
+
+    lane_head = lax.broadcasted_iota(jnp.int32, (tokens, 128), 1) // HEAD_DIM
+    sub_head = lax.broadcasted_iota(jnp.int32, (128, tokens), 0) // HEAD_DIM
+    zero = jnp.zeros((), bf16)
+    span_q = 256
+    scale = 1.0 / math.sqrt(HEAD_DIM)
+
+    def attend(p, carry):
+        q = mixed[:, block(p, 128)] * jnp.asarray(scale, bf16)
+        k = mixed[:, pl.ds(pl.multiple_of(width + p * 128, 128), 128)]
+        v = mixed[:, pl.ds(pl.multiple_of(2 * width + p * 128, 128), 128)]
+        vt = jnp.transpose(v)
+        for c in range(0, tokens, span_q):
+            ct = jnp.zeros((128, span_q), f32)
+            for h in (0, 1):
+                s = dot_nt(k, jnp.where(lane_head == h, q, zero)[c : c + span_q]) + bias[:, c : c + span_q].astype(f32)
+                peak = jnp.max(s, axis=0, keepdims=True)
+                e = jnp.exp(s - peak)
+                total = jnp.sum(e, axis=0, keepdims=True)
+                lse[pl.ds(2 * p + h, 1), c : c + span_q] = peak + jnp.log(total)
+                probs = (e * (1.0 / total)).astype(bf16)
+                ct = ct + dot_nn(jnp.where(sub_head == h, vt, zero), probs)
+            context[c : c + span_q, block(p, 128)] = jnp.transpose(ct).astype(bf16)
+        return carry
+
+    pairs = heads // 2
+    lax.fori_loop(0, pairs // 2, attend, 0)
+    ag["in"].send(3)
+    lax.fori_loop(pairs // 2, pairs, attend, 0)
+    ag["down"].send(2)
+    ag["out"].done()
+
+    for d, spot in enumerate(spots):
+        out_nat[rows * d : rows * d + rows, :] = wout[spot]
+    mid[...] = emb[...] + dot_nt(context[...], out_nat[...])
+    norm_forward(mid, gain_rows[8:9, :], normed_two)
+    ag["in"].last()
+    ag["down"].send(3)
+    ag["in"].done()
+
+    into = win.reshape(hidden, width)
+    down = wdown.reshape(hidden, width)
+    tile = 512
+
+    def expand(j, carry):
+        c = block(j, tile)
+        pre = dot_nt(normed_two[...], into[c, :])
+        phi = 0.5 * lax.erf(pre * math.sqrt(0.5)) + 0.5
+        act[:, c] = (pre * phi).astype(bf16)
+        slope[:, c] = (phi + pre * (jnp.exp(pre * pre * -0.5) * (1.0 / math.sqrt(2.0 * math.pi)))).astype(bf16)
+        return carry
+
+    lax.fori_loop(0, hidden // tile, expand, 0)
+    ag["qkv"].mover.sent()
+    grad_down = wqkv.reshape(hidden, width)
+
+    def down_gradient(j, carry):
+        c = block(j, tile)
+        grad_down[c, :] = dot_tn(act[:, c], cot[...]).astype(bf16)
+        return carry
+
+    lax.fori_loop(0, hidden // tile, down_gradient, 0)
+
+    rs = {}
+    outs = {"down": down_o, "in": in_o, "out": out_o, "qkv": qkv_o, "small": small_o, "gains": gains_o, "table": table_o}
+    parts = {"down": wqkv, "in": wdown, "out": wout, "qkv": win, "small": wsmall, "gains": wgains, "table": wtable}
+    for i, name in enumerate(outs):
+        cut, _, orders = tensors[name]
+        rs[name] = Scatter(
+            g, at, Mover(rs_send.at[i], rs_recv.at[i]), parts[name], outs[name].shape[0], outs[name], cut, orders, bufs[name]
+        )
+    rs["down"].start()
+    ag["down"].last()
+    rs["down"].send(1)
+    ag["down"].done()
+
+    output[...] = (mid[...] + dot_nn(act[...], down[...])).astype(bf16)
+
+    def act_gradient(j, carry):
+        c = block(j, tile)
+        slope[:, c] = (dot_nt(cot[...], down[c, :]) * slope[:, c].astype(f32)).astype(bf16)
+        return carry
+
+    lax.fori_loop(0, hidden // tile, act_gradient, 0)
+    ag["down"].mover.sent()
+
+    def in_gradient(j, carry):
+        c = block(j, tile)
+        down[c, :] = dot_tn(slope[:, c], normed_two[...]).astype(bf16)
+        return carry
+
+    lax.fori_loop(0, hidden // tile, in_gradient, 0)
+    rs["in"].start()
+    rs["down"].send(2)
+    grad_t[...] = dot_nn(slope[...], into[...])
+    rs["in"].send(1)
+    branch, grad_context, grad_emb = pl.ds(0, width), pl.ds(width, width), pl.ds(2 * width, width)
+
+    def put_mid(r, grad):
+        total = cot[r, :].astype(f32) + grad
+        mid[r, :] = total
+        act[r, branch] = total.astype(bf16)
+
+    two_grad = norm_backward(mid, gain_rows[8:9, :], grad_t, put_mid)
+    for s in ("gains", "small", "table", "out", "in"):
+        ag[s].mover.sent()
+    for j in range(2):
+        part = dot_tn(act[:, pl.ds(j * width // 2, width // 2)], context[...])
+        for d in range(len(spots) // 2):
+            wout[spots[j * len(spots) // 2 + d]] = part[rows * d : rows * d + rows].astype(bf16)
+    rs["out"].start()
+    act[:, grad_context] = dot_nn(act[:, branch], out_nat[...]).astype(bf16)
+    rs["out"].send(1)
+
+    def attend_back(p, carry):
+        q = mixed[:, block(p, 128)] * jnp.asarray(scale, bf16)
+        k = mixed[:, pl.ds(pl.multiple_of(width + p * 128, 128), 128)]
+        v = mixed[:, pl.ds(pl.multiple_of(2 * width + p * 128, 128), 128)]
+        gc = act[:, pl.ds(pl.multiple_of(width + p * 128, 128), 128)]
+        kt = jnp.transpose(k)
+        gv = jnp.zeros((tokens, 128), f32)
+        gk = jnp.zeros((tokens, 128), f32)
+        for c in range(0, tokens, span_q):
+            gq = jnp.zeros((128, span_q), f32)
+            for h in (0, 1):
+                qh = jnp.where(lane_head == h, q, zero)[c : c + span_q]
+                gh = jnp.where(lane_head == h, gc, zero)[c : c + span_q]
+                s = dot_nt(k, qh) + bias[:, c : c + span_q].astype(f32)
+                probs = jnp.exp(s - lse[pl.ds(2 * p + h, 1), c : c + span_q])
+                gv = gv + dot_nn(probs.astype(bf16), gh)
+                weighed = probs * dot_nt(v, gh)
+                gs = (weighed - probs * jnp.sum(weighed, axis=0, keepdims=True)).astype(bf16)
+                gk = gk + dot_nn(gs, qh)
+                gq = gq + dot_nn(jnp.where(sub_head == h, kt, zero), gs)
+            mixed[c : c + span_q, block(p, 128)] = jnp.transpose(gq * scale).astype(bf16)
+        mixed[:, pl.ds(pl.multiple_of(width + p * 128, 128), 128)] = gk.astype(bf16)
+        mixed[:, pl.ds(pl.multiple_of(2 * width + p * 128, 128), 128)] = gv.astype(bf16)
+        return carry
+
+    lax.fori_loop(0, pairs // 2, attend_back, 0)
+    rs["down"].send(3)
+    rs["in"].send(2)
+    lax.fori_loop(pairs // 2, pairs, attend_back, 0)
+    rs["in"].send(3)
+    rs["out"].send(2)
+
+    grad_t[...] = dot_nn(mixed[...], qkv_nat[...])
+
+    def qkv_gradient(j, carry):
+        c = block(j, width // 2)
+        qkv_nat[c, :] = dot_tn(mixed[:, c], normed[...]).astype(bf16)
+        return carry
+
+    lax.fori_loop(0, 6, qkv_gradient, 0)
+    for d, spot in enumerate(spots):
+        win[(*spot, pl.ds(0, 3 * rows))] = qkv_nat[3 * rows * d : 3 * rows * (d + 1), :]
+    rs["qkv"].start()
+    rs["out"].send(3)
+
+    def put_emb(r, grad):
+        act[r, grad_emb] = (mid[r, :] + grad).astype(bf16)
+
+    one_grad = norm_backward(emb, gain_rows[0:1, :], grad_t, put_emb)
+    rs["qkv"].send(1)
+    part = dot_tn(act[:, grad_emb], feats[...])
+    for d, spot in enumerate(spots):
+        wsmall[spot] = part[rows * d : rows * d + rows].astype(bf16)
+    rs["small"].start()
+    one_grad = jnp.broadcast_to(jnp.sum(one_grad, axis=0, keepdims=True), (8, width))
+    two_grad = jnp.broadcast_to(jnp.sum(two_grad, axis=0, keepdims=True), (8, width))
+    for d, spot in enumerate(spots):
+        j, shift = (rows * d) // 128, (rows * d) % 128
+        for i, v in enumerate((one_grad, two_grad)):
+            r = v[:, 128 * j : 128 * j + 128]
+            if shift:
+                r = pltpu.roll(r, 128 - shift, axis=1)
+            if shift + rows > 128:
+                r = jnp.where(lane < 128 - shift, r, pltpu.roll(v[:, 128 * j + 128 : 128 * j + 256], 128 - shift, axis=1))
+            wgains[(*spot, pl.ds(8 * i, 8))] = r
+    rs["gains"].start()
+    raw[...] = dot_nn(act[:, grad_emb], small_nat[:, :EMBED])
+    for i in range(groups):
+        r = slice(64 * i, 64 * i + 64)
+        grad = raw[r, :]
+        noise_grad[r, :] = level_s[8 + i : 9 + i, :] * grad
+        raw[r, :] = level_s[i : i + 1, :] * grad
+    grad_rows = raw[...].astype(bf16)
+    ids_all = jnp.broadcast_to(ids_row, (span, tokens))
+
+    def count(i, carry):
+        at_row = (lax.broadcasted_iota(jnp.int32, (span, tokens), 0) + i * span).astype(f32)
+        table[block(i, span), :] = dot_nn(jnp.where(ids_all == at_row, 1.0, 0.0).astype(bf16), grad_rows).astype(bf16)
+        return carry
+
+    lax.fori_loop(0, vocab // span, count, 0)
+    rs["table"].start()
+    rs["small"].send(1)
+    rs["gains"].send(1)
+    rs["qkv"].send(2)
+    rs["table"].send(1)
+    rs["down"].last()
+    rs["in"].last()
+    rs["out"].last()
+    rs["small"].send(2)
+    rs["gains"].send(2)
+    rs["qkv"].send(3)
+    rs["table"].send(2)
+    rs["small"].send(3)
+    rs["gains"].send(3)
+    rs["table"].send(3)
+    for name in ("qkv", "small", "gains", "table"):
+        rs[name].last()
+    table_o[...] = table_o[...] * factor_s[0:1, :]
+    for name in rs:
+        rs[name].mover.sent()
+
+
+def ring_local(
+    g,
+    embed_table,
+    token_ids,
+    time_steps,
+    segment_ids,
+    noise_draw,
+    w_up,
+    w_time,
+    w_qkv,
+    w_out,
+    w_in,
+    w_down,
+    gain_one,
+    gain_two,
+    cotangent,
+):
+    tokens, width = cotangent.shape
+    rows = w_up.shape[1]
+    vocab_rows = embed_table.shape[0]
+    hidden_rows = w_down.shape[0]
+    lanes = ("lane", width // 2)
+    tensors = {
+        "gains": (("row", 8), ZXY, YXZ),
+        "small": (("lane", EMBED), ZXY, YXZ),
+        "table": (("row", vocab_rows // 2), ZXY, YXZ),
+        "qkv": (lanes, ZXY, YXZ),
+        "out": (lanes, ZXY, YXZ),
+        "in": (lanes, ZXY, YXZ),
+        "down": (lanes, XZY, YXZ),
+    }
+    shapes = {
+        "down": (hidden_rows, width, bf16),
+        "in": (hidden_rows, width, bf16),
+        "out": (rows, width, bf16),
+        "qkv": (3 * rows, width, bf16),
+        "small": (rows, 2 * EMBED, bf16),
+        "gains": (16, 128, f32),
+        "table": (vocab_rows, EMBED, bf16),
+    }
+    lead = (g.Z, g.Y, g.X, 2)
+    devices = g.Z * g.F
+    hidden = hidden_rows * devices
+    scratch = [
+        pltpu.VMEM((rows, 2 * EMBED), bf16),
+        pltpu.VMEM((16, 128), f32),
+        pltpu.VMEM((*lead, vocab_rows, EMBED), bf16),
+        pltpu.VMEM((*lead, rows, 2 * EMBED), bf16),
+        pltpu.VMEM((*lead, 16, 128), f32),
+        pltpu.VMEM((*lead, hidden_rows, width), bf16),
+        pltpu.VMEM((*lead, rows, width), bf16),
+        pltpu.VMEM((*lead, hidden_rows, width), bf16),
+        pltpu.VMEM((*lead, hidden_rows, width), bf16),
+        pltpu.VMEM((width, 2 * EMBED), bf16),
+        pltpu.VMEM((3 * width, width), bf16),
+        pltpu.VMEM((width, width), bf16),
+        pltpu.VMEM((16, width), f32),
+        pltpu.VMEM((8, 128), f32),
+        pltpu.VMEM((16, 128), f32),
+        pltpu.VMEM((tokens, 2 * EMBED), bf16),
+        pltpu.VMEM((tokens, width), f32),
+        pltpu.VMEM((tokens, width), bf16),
+        pltpu.VMEM((tokens, 3 * width), bf16),
+        pltpu.VMEM((tokens, width), bf16),
+        pltpu.VMEM((16, tokens), f32),
+        pltpu.VMEM((tokens, width), f32),
+        pltpu.VMEM((tokens, width), bf16),
+        pltpu.VMEM((tokens, hidden), bf16),
+        pltpu.VMEM((tokens, hidden), bf16),
+        pltpu.VMEM((tokens, width), f32),
+        pltpu.VMEM((tokens, EMBED), f32),
+        pltpu.VMEM((tokens, tokens), bf16),
+    ]
+    for name, (r, c, dtype) in shapes.items():
+        cut, _, orders = tensors[name]
+        scratch += scatter_buffers(g, r, c, cut, orders, dtype)
+    n = len(shapes)
+    scratch += [pltpu.SemaphoreType.DMA((n,))]
+    scratch += [pltpu.SemaphoreType.DMA((n, gather_copies(g)))] * 2
+    scratch += [pltpu.SemaphoreType.DMA((n, scatter_copies(g)))] * 2
+    vm, sm = pl.BlockSpec(memory_space=pltpu.VMEM), pl.BlockSpec(memory_space=pltpu.SMEM)
+    shard = lambda name: jax.ShapeDtypeStruct(shapes[name][:2], f32)
+    outs = pl.pallas_call(
+        functools.partial(layer_kernel, g, tensors),
+        out_shape=(
+            jax.ShapeDtypeStruct((tokens, width), bf16),
+            jax.ShapeDtypeStruct((tokens, EMBED), f32),
+            *[shard(name) for name in ("table", "small", "qkv", "out", "in", "down", "gains")],
+        ),
+        in_specs=[vm] * 10 + [sm] * 2 + [vm] * 2,
+        out_specs=(vm,) * 9,
+        scratch_shapes=scratch,
+        compiler_params=pltpu.CompilerParams(
+            collective_id=0, has_side_effects=True, vmem_limit_bytes=67043328
+        ),
+        name="layer",
+    )(
+        embed_table,
+        w_up.T,
+        w_time.T,
+        w_qkv.T,
+        w_out.T,
+        w_in.T,
+        w_down,
+        gain_one.reshape(1, rows),
+        gain_two.reshape(1, rows),
+        token_ids.reshape(1, tokens),
+        time_steps,
+        segment_ids,
+        noise_draw,
+        cotangent,
+    )
+    output, noise_grad, table_own, small_own, qkv_own, out_own, in_own, down_own, gains_own = outs
+    return (
+        output,
+        table_own,
+        noise_grad,
+        small_own[:, :EMBED].T,
+        small_own[:, EMBED:].T,
+        qkv_own.T,
+        out_own.T,
+        in_own.T,
+        down_own,
+        gains_own[0, :rows],
+        gains_own[8, :rows],
+    )
+
+
 def solution(mesh):
     in_specs = (
         P(("dp", "fsdp"), None),
@@ -263,4 +1027,11 @@
         P(("dp", "fsdp")),
         P(("dp", "fsdp")),
     )
+    grid = Grid(mesh.shape["dp"], mesh.shape["fsdp"])
+
+    def local(*args):
+        if all(rows % 8 == 0 for rows in (args[5].shape[1], args[10].shape[0])):
+            return ring_local(grid, *args)
+        return native_local(*args)
+
     return jax.shard_map(local, mesh=mesh, in_specs=in_specs, out_specs=out_specs, check_vma=False)

time: 1250 us -> 213 us (0.17)
  waiting for transfers between devices: 868 us -> 0 us
  Pallas kernels: 0 us -> 202 us
  blocking collectives: 202 us -> 0 us
  matrix products: 108 us -> 0 us
  other arithmetic: 30.7 us -> 0 us
  between operations: 15.8 us -> 0.67 us
  local copies, waits for them, and re-layouts: 24 us -> 9.98 us
    reduce_scatter x5 -> x0, waiting for transfers between devices: 569 us -> none  [the longest x1 142 us: local(): lax.psum_scatter(grad_in, ('dp', 'fsdp'), scatter_dimension=1, tiled=True)]
    pallas_call x0 -> x1, Pallas kernels: none -> 202 us  [ring_local(): pl.pallas_call(functools.partial(layer_kernel, g, tensors), out_shape=(ja...]
    unnamed x14 -> x0, waiting for transfers between devices: 199 us -> none
    dot_general x23 -> x0, matrix products: 108 us -> none  [the longest x6 28.8 us: matmul_left(): lax.dot_general(left, right, (((0,), (0,)), ((), ())), preferred_element_...]
    all_gather x5 -> x0, waiting for transfers between devices: 99.9 us -> none  [the longest x1 57.3 us: local(): lax.all_gather(w_down, ('dp', 'fsdp'), axis=0, tiled=True)]
    unnamed x2 -> x0, blocking collectives: 79.9 us -> none
    all_gather x2 -> x0, blocking collectives: 79.4 us -> none  [the longest x1 41.9 us: local(): lax.all_gather(w_up, ('dp', 'fsdp'), axis=1, tiled=True)]
    psum x1 -> x0, blocking collectives: 42.3 us -> none  [local(): norm_total = lax.psum(jnp.sum(norm_values), ('dp', 'fsdp'))]
  transfers between devices with their start and end apart: 12 -> 0, of which waited for: 9 -> 0; matrix products, arithmetic and copies ran while one was open for 7% -> 0% of each run, Pallas kernels for 0% -> 0%
where the time goes in v2:
time: 213 us
  Pallas kernels  202 us (95%)
  local copies, waits for them, and re-layouts  9.98 us (5%)
    pallas_call x1, Pallas kernels, ring_local(): pl.pallas_call(functools.partial(layer_kernel, g, tensors), out_shape=(ja...  202 us
    unnamed x19, local copies, waits for them, and re-layouts  7.45 us

profile of v2, /device:TPU:0, one launch (start us, length us, event | category | flops | bytes accessed | tf_op | source)
XLA Modules:
  0.0 213.1 jit_solution(7332090922481792680)
XLA Ops:
  0.6 202.4 %layer.1 = (bf16[512,768]{1,0:T(8,128)(2,1)}, f32[512,128]{1,0:T(8,128)}, f32[256,128]{1,0:T(8,128)}, f32[24,256]{1,0:T(8,128)}, f32[72,768]{1,0:T(8,128)}, /*in...) custom-call(bf16[256,128]{1,0:T(8,128)(2,1)} %refs_0_.1, bf16[24,128]{1,0:T(8,128)(2,1)} %bitcast.25, ...), custom_call_target="tpu_custom_call" | custom-call | tf_op jit(solution)/shard_map/layer/pallas_call | solution.py:954
  203.1 1.3 slice_bitcast_fusion
  204.4 1.2 slice_bitcast_fusion.2
  205.6 0.0 copy-start.4
  205.6 2.1 copy.32
  207.7 0.0 copy-done.4
  207.7 0.0 copy-start.2
  207.7 0.7 copy.33
  208.4 0.3 copy-done.2
  208.7 0.0 copy-start.3
  208.7 0.7 copy.34
  209.4 0.3 copy-done.3
  209.7 0.0 copy-start.5
  209.7 0.0 copy-start.1
  209.7 0.7 copy.35
  210.4 0.2 copy-done.5
  210.7 0.6 copy.36
  211.3 0.0 copy-done.1
  211.3 0.0 copy-start
  211.3 0.7 copy.37
  212.0 0.4 copy-done
  212.4 0.7 copy.38
Async XLA Ops:
  205.6 2.1 copy-start.4
  207.7 1.0 copy-start.2
  208.7 1.0 copy-start.3
  209.7 0.9 copy-start.5
  209.7 1.5 copy-start.1
  211.3 1.1 copy-start
